TPU v7x, 128 devices: a whole 4x4x4 slice. The times are simulated.
128 devices in a mesh: ctx: 32 (over y, z, core), mp: 4 (over x).
Axes of the slice: x: 4, y: 4, z: 4, core: 2. Of those that a mesh axis runs over, the one named last changes fastest.
Arguments:
- queries: bfloat16 [16384, 4096], P('ctx', 'mp'), may hold values from -15 to 15
- keys: bfloat16 [16384, 2048], P('ctx', 'mp'), may hold values from -15 to 15
- values: bfloat16 [16384, 2048], P('ctx', 'mp'), may hold values from -6 to 6
- grad_out: bfloat16 [16384, 4096], P(('ctx', 'mp')), may hold values from -6 to 6
- band_mask: int32 [128, 9], replicated, may hold values from 0 to 1, as said below
- segment_ids: int32 [16384], replicated, may hold values from 0 to 15, never falling along the last dimension, each value on 1 to 4096 neighbouring positions
Outputs:
- attn_out: bfloat16 [16384, 4096], P(('ctx', 'mp'))
- grad_queries: bfloat16 [16384, 4096], P('ctx', 'mp')
- grad_keys: bfloat16 [16384, 2048], P('ctx', 'mp')
- grad_values: bfloat16 [16384, 2048], P('ctx', 'mp')
Inputs may be any that keep to these rules, and one draw needn't show every extreme that they name: band_mask[b, o] is 1 when query block b may see the key block o blocks before it; offset 0 is always 1. `segment_ids`: segment numbers never fall along the sequence.
All inputs are finite; a program needn't handle non-finite values.
Results may differ from a plain program's by a relative error of at most 0.03.
Values may be sent and summed in bfloat16 or wider, within the bound.
A program may use at most 128 MiB of HBM per device.

v0:
```python
import jax
import jax.numpy as jnp
from jax import lax
from jax.sharding import PartitionSpec as P

Q_HEADS = 32
KV_HEADS = 16
HEAD = 128
WINDOW = 1024
BLOCK = 128


ATTN_SCALE = 168.0 ** (-0.5)
NEG_FILL = -1e30


def shifted(block, axis, distance):
    devices = range(lax.axis_size(axis))
    route = [(i - distance, i) for i in devices if i - distance in devices]
    return lax.ppermute(block, axis, route)


def block_mask(seg_query, seg_key, band_row):
    rows_query = seg_query.shape[0]
    width_keys = seg_key.shape[0]
    distance = WINDOW + jnp.arange(rows_query)[:, None] - jnp.arange(width_keys)[None, :]
    allowed = jnp.repeat(band_row[::-1], BLOCK)
    return (
        (distance >= 0)
        & (distance < WINDOW)
        & (seg_query[:, None] == seg_key[None, :])
        & (allowed[None, :] == 1)
    )


def masked_scores(query_blk, key_slab, valid):
    scores = (
        jnp.einsum("qkgd,skd->kgqs", query_blk, key_slab, preferred_element_type=jnp.float32)
        * ATTN_SCALE
    )
    return jnp.where(valid, scores, NEG_FILL)


def rows_for(reach, local_rows):
    first_row = max(WINDOW - reach * local_rows, 0)
    return WINDOW - (reach - 1) * local_rows - first_row


def body(queries, keys, values, grad_out, band_mask, segment_ids):
    local_rows = queries.shape[0]
    kv_local = keys.shape[1] // HEAD
    q_per_kv = Q_HEADS // KV_HEADS
    span_keys = WINDOW + BLOCK
    block_count = local_rows // BLOCK
    hop_total = (WINDOW + local_rows - 1) // local_rows
    position = lax.axis_index("ctx")
    stacked = jnp.stack([keys, values])
    portions = []
    for reach in range(hop_total, 0, -1):
        needed = rows_for(reach, local_rows)
        received = shifted(stacked, "ctx", reach)
        portions.append(received)
    extended = jnp.concatenate(portions + [stacked], axis=1)
    key_ext = extended[0].reshape(WINDOW + local_rows, kv_local, HEAD)
    value_ext = extended[1].reshape(WINDOW + local_rows, kv_local, HEAD)
    seg_padded = jnp.concatenate([jnp.full((WINDOW,), -1, jnp.int32), segment_ids])
    seg_ext = lax.dynamic_slice_in_dim(seg_padded, position * local_rows, WINDOW + local_rows, 0)
    seg_local = lax.dynamic_slice_in_dim(segment_ids, position * local_rows, local_rows, 0)
    band_local = lax.dynamic_slice_in_dim(band_mask, position * block_count, block_count, 0)
    grad_heads = lax.all_to_all(grad_out, "mp", split_axis=1, concat_axis=0, tiled=True)

    def block_inputs(block_idx):
        start = block_idx * BLOCK
        query_blk = lax.dynamic_slice_in_dim(queries, start, BLOCK, 0).reshape(
            BLOCK, kv_local, q_per_kv, HEAD
        )
        key_slab = lax.dynamic_slice_in_dim(key_ext, start, span_keys, 0)
        value_slab = lax.dynamic_slice_in_dim(value_ext, start, span_keys, 0)
        seg_query = lax.dynamic_slice_in_dim(seg_local, start, BLOCK, 0)
        seg_key = lax.dynamic_slice_in_dim(seg_ext, start, span_keys, 0)
        band_row = lax.dynamic_index_in_dim(band_local, block_idx, 0, keepdims=False)
        return (query_blk, key_slab, value_slab, block_mask(seg_query, seg_key, band_row))

    def forward_step(carry, block_idx):
        query_blk, key_slab, value_slab, valid = block_inputs(block_idx)
        scores = masked_scores(query_blk, key_slab, valid)
        row_max = jnp.max(scores, axis=-1, keepdims=True)
        log_norm = row_max + jnp.log(jnp.sum(jnp.exp(scores - row_max), axis=-1, keepdims=True))
        prob_bf = jnp.exp(scores - log_norm).astype(jnp.bfloat16)
        attended = jnp.einsum(
            "kgqs,skd->qkgd", prob_bf, value_slab, preferred_element_type=jnp.float32
        ).astype(jnp.bfloat16)
        attended = attended.reshape(BLOCK, kv_local * q_per_kv * HEAD)
        return (carry, (attended, log_norm))

    block_ids = jnp.arange(block_count, dtype=jnp.int32)
    unused, saved = lax.scan(forward_step, jnp.int32(0), block_ids)
    attn_out = lax.all_to_all(
        saved[0].reshape(local_rows, -1), "mp", split_axis=0, concat_axis=1, tiled=True
    )

    def backward_step(carry, inputs):
        key_grad, value_grad = carry
        block_idx = inputs[0]
        query_blk, key_slab, value_slab, valid = block_inputs(block_idx)
        prob_bf = jnp.exp(masked_scores(query_blk, key_slab, valid) - inputs[2]).astype(
            jnp.bfloat16
        )
        start = block_idx * BLOCK
        grad_blk = lax.dynamic_slice_in_dim(grad_heads, start, BLOCK, 0).reshape(
            BLOCK, kv_local, q_per_kv, HEAD
        )
        attended_blk = inputs[1].reshape(BLOCK, kv_local, q_per_kv, HEAD)
        delta = jnp.sum(
            grad_blk.astype(jnp.float32) * attended_blk.astype(jnp.float32), axis=-1
        ).transpose(1, 2, 0)[..., None]
        value_part = jnp.einsum(
            "kgqs,qkgd->skd", prob_bf, grad_blk, preferred_element_type=jnp.float32
        )
        grad_prob = jnp.einsum(
            "qkgd,skd->kgqs", grad_blk, value_slab, preferred_element_type=jnp.float32
        )
        grad_score = (prob_bf.astype(jnp.float32) * (grad_prob - delta)).astype(jnp.bfloat16)
        grad_query = (
            jnp.einsum("kgqs,skd->qkgd", grad_score, key_slab, preferred_element_type=jnp.float32)
            * ATTN_SCALE
        )
        grad_query = grad_query.astype(jnp.bfloat16).reshape(BLOCK, kv_local * q_per_kv * HEAD)
        key_part = (
            jnp.einsum("kgqs,qkgd->skd", grad_score, query_blk, preferred_element_type=jnp.float32)
            * ATTN_SCALE
        )
        key_grad = lax.dynamic_update_slice_in_dim(
            key_grad, lax.dynamic_slice_in_dim(key_grad, start, span_keys, 0) + key_part, start, 0
        )
        value_grad = lax.dynamic_update_slice_in_dim(
            value_grad,
            lax.dynamic_slice_in_dim(value_grad, start, span_keys, 0) + value_part,
            start,
            0,
        )
        return ((key_grad, value_grad), grad_query)

    zeros = jnp.zeros((WINDOW + local_rows, kv_local, HEAD), jnp.float32)
    (key_grad, value_grad), grad_blocks = lax.scan(
        backward_step, (zeros, zeros), (block_ids,) + tuple(saved)
    )
    grad_queries = grad_blocks.reshape(local_rows, -1)
    both_grads = jnp.stack([key_grad, value_grad])
    owned = both_grads[:, WINDOW:]
    for reach in range(1, hop_total + 1):
        first_row = max(WINDOW - reach * local_rows, 0)
        last_row = WINDOW - (reach - 1) * local_rows
        needed = last_row - first_row
        returned = shifted(both_grads[:, first_row:last_row], "ctx", -reach)
        owned = owned.at[:, local_rows - needed :].add(returned)
    grad_keys = owned[0].reshape(local_rows, -1).astype(jnp.bfloat16)
    grad_values = owned[1].reshape(local_rows, -1).astype(jnp.bfloat16)
    return (attn_out, grad_queries, grad_keys, grad_values)


def solution(mesh):
    placed = (P("ctx", "mp"), P("ctx", "mp"), P("ctx", "mp"), P(("ctx", "mp"), None), P(), P())
    return jax.shard_map(
        body,
        mesh=mesh,
        in_specs=placed,
        out_specs=(P(("ctx", "mp"), None), P("ctx", "mp"), P("ctx", "mp"), P("ctx", "mp")),
        check_vma=False,
    )
```

profile of v0, /device:TPU:96, one launch (start us, length us, event | category | flops | bytes accessed | tf_op | source)
XLA Modules:
  0.0 265.7 jit_solution(17010820344281772029)
XLA Ops:
  0.7 1.3 copy.75
  2.0 1.3 copy.76
  3.3 1.1 pad_maximum_fusion.1
  4.3 2.2 collective-permute-start
  6.6 1.9 collective-permute-start.1
  8.5 1.3 copy.81
  9.8 4.4 %all-to-all-start.1 = ((bf16[128,4,1024]{0,2,1:T(8,128)(2,1)}), bf16[128,4,1024]{0,2,1:T(8,128)(2,1)S(1)}, u32[]{:S(2)}, u32[]{:S(2)}) async-start(bf16[128,4,1024]{0,2,1:T(8,128)(2,1)} %bitcast.41), calls=%async_computation.1 | async-start | bytes 2097152 | tf_op jit(solution)/shard_map/all_to_all | solution.py:70
  14.4 1.3 copy.79
  15.9 14.1 %all-to-all-done.1 = bf16[128,4,1024]{0,2,1:T(8,128)(2,1)S(1)} async-done(((bf16[128,4,1024]{0,2,1:T(8,128)(2,1)}), bf16[128,4,1024]{0,2,1:T(8,128)(2,1)S(1)}, u32[]{:S(2)}, u32[]{:S(2)}) %all-to-all-start.1) | async-done | bytes 1048608 | tf_op jit(solution)/shard_map/all_to_all | solution.py:70
  30.0 1.3 copy.82
  31.3 1.4 collective-permute-done
  32.7 10.1 %collective-permute-done.1 = bf16[2,512,512]{1,2,0:T(8,128)(2,1)} collective-permute-done((bf16[2,512,512]{1,2,0:T(8,128)(2,1)}, bf16[2,512,512]{1,2,0:T(8,128)(2,1)}, u32[]{:S(2)}, u32[]{:S(2)}) %collective-permute-start.1) | collective-permute-done | bytes 1048608 | tf_op jit(solution)/shard_map/ppermute | solution.py:20
  42.8 1.6 maximum_maximum_fusion
  44.4 1.4 fusion.49
  45.8 1.7 copy.78
  47.5 44.3 %while.30 = (s32[]{:T(128)}, bf16[4,128,1024]{1,2,0:T(8,128)(2,1)}, f32[4,4,2,128,1]{3,2,1,4,0:T(2,128)S(1)}, s32[4]{0:T(128)S(1)}, bf16[1536,4,128]{0,2,1:T(8,1...) while((s32[]{:T(128)}, bf16[4,128,1024]{1,2,0:T(8,128)(2,1)}, ...), condition=%wide.region_3.4_spmd, body=%wide.region_0.3_spmd.sunk | while | flops 613399680 | bytes 18435308 | solution.py:97
  51.8 1.0 constant_dynamic-slice_fusion.11
  52.8 2.1 fusion.87
  55.6 2.2 fusion.88
  62.9 1.0 constant_dynamic-slice_fusion.11
  63.9 2.1 fusion.87
  66.6 2.2 fusion.88
  74.0 1.0 constant_dynamic-slice_fusion.11
  74.9 2.1 fusion.87
  77.7 2.2 fusion.88
  85.0 1.0 constant_dynamic-slice_fusion.11
  86.0 2.1 fusion.87
  88.8 2.2 fusion.88
  91.7 2.0 broadcast_in_dim.48
  93.7 2.1 broadcast_in_dim.48.clone
  95.8 86.1 %while.31 = (s32[]{:T(128)}, f32[1536,4,128]{0,2,1:T(8,128)}, f32[1536,4,128]{0,2,1:T(8,128)}, bf16[4,128,1024]{2,1,0:T(8,128)(2,1)}, s32[4]{0:T(128)S(1)}, /*in...) while((s32[]{:T(128)}, f32[1536,4,128]{0,2,1:T(8,128)}, ...), condition=%wide.region_6.7_spmd, body=%wide.region_4.6_spmd.sunk | while | flops 1522973824 | bytes 57613656 | solution.py:145
  100.2 1.0 constant_dynamic-slice_fusion.12
  101.2 2.6 fusion.101
  106.0 2.4 fusion.103
  108.5 1.1 fusion.104
  109.6 2.8 %fusion.106 = bf16[4,128,2,128]{3,1,2,0:T(8,128)(2,1)S(1)} fusion(bf16[4,2,128,1152]{2,3,1,0:T(8,128)(2,1)S(1)} %fusion.103, bf16[1536,4,128]{2,0,1:T(8,128)(2,1)} %get-tuple-element.581, s32[]{:T(128)S(6)} %select_n.68), kind=kOutput, calls=%fused_computation.45.clone.1 | convolution fusion | flops 302252032 | bytes 3801092 | tf_op jit(solution)/shard_map/while/body/eval_jaxpr/kgqs,skd->qkgd/dot_general | solution.py:125
  113.3 4.0 %fusion.105 = f32[1536,4,128]{0,2,1:T(8,128)} fusion(f32[1536,4,128]{0,2,1:T(8,128)} %get-tuple-element.554, s32[]{:T(128)S(6)} %select_n.68, bf16[128,4,2,128]{0,3,2,1:T(8,128)(2,1)S(1)} %bitcast.194, bf16[4,2,128,1152]{2,3,1,0:T(8,128)(2,1)S(1)} %fusion.101), kind=kOutput, calls=%fused_computation.38.clone.1 | convolution fusion | flops 302579712 | bytes 7340036 | tf_op jit(solution)/shard_map/while/body/eval_jaxpr/kgqs,qkgd->skd/dot_general | solution.py:117
  121.7 1.0 constant_dynamic-slice_fusion.12
  122.7 2.6 fusion.101
  127.5 2.5 fusion.103
  130.0 1.1 fusion.104
  131.1 2.8 %fusion.106 = bf16[4,128,2,128]{3,1,2,0:T(8,128)(2,1)S(1)} fusion(bf16[4,2,128,1152]{2,3,1,0:T(8,128)(2,1)S(1)} %fusion.103, bf16[1536,4,128]{2,0,1:T(8,128)(2,1)} %get-tuple-element.581, s32[]{:T(128)S(6)} %select_n.68), kind=kOutput, calls=%fused_computation.45.clone.1 | convolution fusion | flops 302252032 | bytes 3801092 | tf_op jit(solution)/shard_map/while/body/eval_jaxpr/kgqs,skd->qkgd/dot_general | solution.py:125
  134.8 4.0 %fusion.105 = f32[1536,4,128]{0,2,1:T(8,128)} fusion(f32[1536,4,128]{0,2,1:T(8,128)} %get-tuple-element.554, s32[]{:T(128)S(6)} %select_n.68, bf16[128,4,2,128]{0,3,2,1:T(8,128)(2,1)S(1)} %bitcast.194, bf16[4,2,128,1152]{2,3,1,0:T(8,128)(2,1)S(1)} %fusion.101), kind=kOutput, calls=%fused_computation.38.clone.1 | convolution fusion | flops 302579712 | bytes 7340036 | tf_op jit(solution)/shard_map/while/body/eval_jaxpr/kgqs,qkgd->skd/dot_general | solution.py:117
  143.2 1.0 constant_dynamic-slice_fusion.12
  144.2 2.6 fusion.101
  149.0 2.5 fusion.103
  151.5 1.1 fusion.104
  152.6 2.8 %fusion.106 = bf16[4,128,2,128]{3,1,2,0:T(8,128)(2,1)S(1)} fusion(bf16[4,2,128,1152]{2,3,1,0:T(8,128)(2,1)S(1)} %fusion.103, bf16[1536,4,128]{2,0,1:T(8,128)(2,1)} %get-tuple-element.581, s32[]{:T(128)S(6)} %select_n.68), kind=kOutput, calls=%fused_computation.45.clone.1 | convolution fusion | flops 302252032 | bytes 3801092 | tf_op jit(solution)/shard_map/while/body/eval_jaxpr/kgqs,skd->qkgd/dot_general | solution.py:125
  156.4 4.0 %fusion.105 = f32[1536,4,128]{0,2,1:T(8,128)} fusion(f32[1536,4,128]{0,2,1:T(8,128)} %get-tuple-element.554, s32[]{:T(128)S(6)} %select_n.68, bf16[128,4,2,128]{0,3,2,1:T(8,128)(2,1)S(1)} %bitcast.194, bf16[4,2,128,1152]{2,3,1,0:T(8,128)(2,1)S(1)} %fusion.101), kind=kOutput, calls=%fused_computation.38.clone.1 | convolution fusion | flops 302579712 | bytes 7340036 | tf_op jit(solution)/shard_map/while/body/eval_jaxpr/kgqs,qkgd->skd/dot_general | solution.py:117
  165.7 2.6 fusion.101
  170.5 2.5 fusion.103
  173.0 1.1 fusion.104
  174.1 2.8 %fusion.106 = bf16[4,128,2,128]{3,1,2,0:T(8,128)(2,1)S(1)} fusion(bf16[4,2,128,1152]{2,3,1,0:T(8,128)(2,1)S(1)} %fusion.103, bf16[1536,4,128]{2,0,1:T(8,128)(2,1)} %get-tuple-element.581, s32[]{:T(128)S(6)} %select_n.68), kind=kOutput, calls=%fused_computation.45.clone.1 | convolution fusion | flops 302252032 | bytes 3801092 | tf_op jit(solution)/shard_map/while/body/eval_jaxpr/kgqs,skd->qkgd/dot_general | solution.py:125
  177.9 4.0 %fusion.105 = f32[1536,4,128]{0,2,1:T(8,128)} fusion(f32[1536,4,128]{0,2,1:T(8,128)} %get-tuple-element.554, s32[]{:T(128)S(6)} %select_n.68, bf16[128,4,2,128]{0,3,2,1:T(8,128)(2,1)S(1)} %bitcast.194, bf16[4,2,128,1152]{2,3,1,0:T(8,128)(2,1)S(1)} %fusion.101), kind=kOutput, calls=%fused_computation.38.clone.1 | convolution fusion | flops 302579712 | bytes 7340036 | tf_op jit(solution)/shard_map/while/body/eval_jaxpr/kgqs,qkgd->skd/dot_general | solution.py:117
  181.9 4.8 %fusion.43 = (f32[2,512,4,128]{1,3,2,0:T(8,128)}, f32[2,512,4,128]{1,3,2,0:T(8,128)}) fusion(f32[1,1536,4,128]{1,3,2,0:T(8,128)} %bitcast.189, f32[1,1536,4,128]{1,3,2,0:T(8,128)} %bitcast.191), kind=kLoop, calls=%fused_computation.78 | loop fusion | flops 1048576 | bytes 10485760 | tf_op jit(solution)/shard_map/stack | solution.py:149
  186.7 2.2 collective-permute-start.2
  188.9 2.3 collective-permute-start.3
  191.2 20.1 %all_to_all.35 = bf16[4,128,1024]{1,2,0:T(8,128)(2,1)} all-to-all(bf16[4,128,1024]{1,2,0:T(8,128)(2,1)} %get-tuple-element.545), channel_id=1, replica_groups=mesh['ctx'=32,'mp'=4] {'mp'}, dimensions={0} | all-to-all | bytes 2097152 | tf_op jit(solution)/shard_map/all_to_all | solution.py:98
  211.3 2.3 copy.106
  213.6 19.8 %collective-permute-done.2 = f32[2,512,4,128]{1,3,2,0:T(8,128)} collective-permute-done((f32[2,512,4,128]{1,3,2,0:T(8,128)}, f32[2,512,4,128]{1,3,2,0:T(8,128)}, u32[]{:S(2)}, u32[]{:S(2)}) %collective-permute-start.2) | collective-permute-done | bytes 2097184 | tf_op jit(solution)/shard_map/ppermute | solution.py:20
  233.4 27.2 %collective-permute-done.3 = f32[2,512,4,128]{1,3,2,0:T(8,128)} collective-permute-done((f32[2,512,4,128]{1,3,2,0:T(8,128)}, f32[2,512,4,128]{1,3,2,0:T(8,128)}, u32[]{:S(2)}, u32[]{:S(2)}) %collective-permute-start.3) | collective-permute-done | bytes 2097184 | tf_op jit(solution)/shard_map/ppermute | solution.py:20
  260.6 3.1 %fusion.47 = bf16[2,512,4,128]{1,3,2,0:T(8,128)(2,1)S(1)} fusion(f32[2,512,4,128]{1,3,2,0:T(8,128)} %collective-permute-done.3, f32[2,512,4,128]{1,3,2,0:T(8,128)} %collective-permute-done.2, f32[1,1536,4,128]{1,3,2,0:T(8,128)S(1)} %bitcast.190, f32[1,1536,4,128]{1,3,2,0:T(8,128)} %bitcast.192), kind=kLoop, calls=%fused_computation.82 | loop fusion | flops 2097152 | bytes 11534336 | tf_op jit(solution)/shard_map/convert.2
  263.7 1.0 copy.107
  264.7 1.0 copy.108
  (149 shorter events, 33.8 us)
Async XLA Ops:
  0.6 13.6 %copy-start = (s32[128,9]{0,1:T(8,128)S(1)}, s32[128,9]{0,1:T(8,128)}, u32[]{:S(2)}) copy-start(s32[128,9]{0,1:T(8,128)} %param.22) | copy-start | bytes 13828
  0.6 7.9 %copy-start.4 = (bf16[128,4096]{1,0:T(8,128)(2,1)S(1)}, bf16[128,4096]{1,0:T(8,128)(2,1)}, u32[]{:S(2)}) copy-start(bf16[128,4096]{1,0:T(8,128)(2,1)} %param.21) | copy-start | bytes 3145732
  4.3 10.1 %copy-start.5 = (bf16[512,1024]{1,0:T(8,128)(2,1)S(1)}, bf16[512,1024]{1,0:T(8,128)(2,1)}, u32[]{:S(2)}) copy-start(bf16[512,1024]{1,0:T(8,128)(2,1)} %param.18) | copy-start | bytes 3145732
  4.3 28.4 %collective-permute-start = (bf16[2,512,512]{1,2,0:T(8,128)(2,1)}, bf16[2,512,512]{1,2,0:T(8,128)(2,1)}, u32[]{:S(2)}, u32[]{:S(2)}) collective-permute-start(bf16[2,512,512]{1,2,0:T(8,128)(2,1)} %pad_maximum_fusion.1), channel_id=1, source_target_pairs={{0,8},{4,12},{8,16},{12,20},{16,24},{20,28},{24,32},{28,36},{32,40... | collective-permute-start | bytes 3145736 | tf_op jit(solution)/shard_map/ppermute | solution.py:20
  6.6 36.2 %collective-permute-start.1 = (bf16[2,512,512]{1,2,0:T(8,128)(2,1)}, bf16[2,512,512]{1,2,0:T(8,128)(2,1)}, u32[]{:S(2)}, u32[]{:S(2)}) collective-permute-start(bf16[2,512,512]{1,2,0:T(8,128)(2,1)} %pad_maximum_fusion.1), channel_id=1, source_target_pairs={{0,4},{4,8},{8,12},{12,16},{16,20},{20,24},{24,28},{28,32},{32,36}... | collective-permute-start | bytes 3145736 | tf_op jit(solution)/shard_map/ppermute | solution.py:20
  9.8 5.9 %copy-start.6 = (s32[16384]{0:T(1024)S(1)}, s32[16384]{0:T(1024)}, u32[]{:S(2)}) copy-start(s32[16384]{0:T(1024)} %param.23) | copy-start | bytes 196612
  9.8 20.2 %all-to-all-start.1 = ((bf16[128,4,1024]{0,2,1:T(8,128)(2,1)}), bf16[128,4,1024]{0,2,1:T(8,128)(2,1)S(1)}, u32[]{:S(2)}, u32[]{:S(2)}) async-start(bf16[128,4,1024]{0,2,1:T(8,128)(2,1)} %bitcast.41), calls=%async_computation.1 | async-start | bytes 2097152 | tf_op jit(solution)/shard_map/all_to_all | solution.py:70
  106.0 2.5 copy-start.1
  109.6 2.9 %copy-start.2 = (f32[1536,4,128]{0,2,1:T(8,128)}, f32[1536,4,128]{0,2,1:T(8,128)S(1)}, u32[]{:S(2)}) copy-start(f32[1536,4,128]{0,2,1:T(8,128)S(1)} %fusion.104) | copy-start | bytes 9437188 | tf_op jit(solution)/shard_map/while
  127.5 2.5 copy-start.1
  131.1 2.9 %copy-start.2 = (f32[1536,4,128]{0,2,1:T(8,128)}, f32[1536,4,128]{0,2,1:T(8,128)S(1)}, u32[]{:S(2)}) copy-start(f32[1536,4,128]{0,2,1:T(8,128)S(1)} %fusion.104) | copy-start | bytes 9437188 | tf_op jit(solution)/shard_map/while
  149.0 2.5 copy-start.1
  152.6 2.9 %copy-start.2 = (f32[1536,4,128]{0,2,1:T(8,128)}, f32[1536,4,128]{0,2,1:T(8,128)S(1)}, u32[]{:S(2)}) copy-start(f32[1536,4,128]{0,2,1:T(8,128)S(1)} %fusion.104) | copy-start | bytes 9437188 | tf_op jit(solution)/shard_map/while
  170.5 2.5 copy-start.1
  174.1 2.9 %copy-start.2 = (f32[1536,4,128]{0,2,1:T(8,128)}, f32[1536,4,128]{0,2,1:T(8,128)S(1)}, u32[]{:S(2)}) copy-start(f32[1536,4,128]{0,2,1:T(8,128)S(1)} %fusion.104) | copy-start | bytes 9437188 | tf_op jit(solution)/shard_map/while
  186.7 73.8 %copy-start.3 = (f32[1536,4,128]{0,2,1:T(8,128)S(1)}, f32[1536,4,128]{0,2,1:T(8,128)}, u32[]{:S(2)}) copy-start(f32[1536,4,128]{0,2,1:T(8,128)} %get-tuple-element.174) | copy-start | bytes 9437188
  186.7 46.7 %collective-permute-start.2 = (f32[2,512,4,128]{1,3,2,0:T(8,128)}, f32[2,512,4,128]{1,3,2,0:T(8,128)}, u32[]{:S(2)}, u32[]{:S(2)}) collective-permute-start(f32[2,512,4,128]{1,3,2,0:T(8,128)} %get-tuple-element.324), channel_id=1, source_target_pairs={{4,0},{8,4},{12,8},{16,12},{20,16},{24,20},{28,24},{32,28},{36,32}... | collective-permute-start | bytes 6291464 | tf_op jit(solution)/shard_map/ppermute | solution.py:20
  188.9 71.6 %collective-permute-start.3 = (f32[2,512,4,128]{1,3,2,0:T(8,128)}, f32[2,512,4,128]{1,3,2,0:T(8,128)}, u32[]{:S(2)}, u32[]{:S(2)}) collective-permute-start(f32[2,512,4,128]{1,3,2,0:T(8,128)} %get-tuple-element.325), channel_id=1, source_target_pairs={{8,0},{12,4},{16,8},{20,12},{24,16},{28,20},{32,24},{36,28},{40,32... | collective-permute-start | bytes 6291464 | tf_op jit(solution)/shard_map/ppermute | solution.py:20
where the time goes:
time: 268 us; the launch traced here: 266 us
  waiting for transfers between devices  72.6 us (27%)
  matrix products  69.1 us (26%)
  local copies, waits for them, and re-layouts  48.6 us (18%)
  loops' own time  21.1 us (8%)
  other arithmetic  20.5 us (8%)
  blocking collectives  20.1 us (8%)
  starting transfers between devices  13.1 us (5%)
    ppermute x4, waiting for transfers between devices, shifted(): return lax.ppermute(block, axis, route)  58.5 us
    all_to_all x1, blocking collectives, body(): lax.all_to_all(saved[0].reshape(local_rows, -1), 'mp', split_axis=0, conc...  20.1 us
    dot_general x8, matrix products, masked_scores(): jnp.einsum('qkgd,skd->kgqs', query_blk, key_slab, preferred_element_type=...  18.6 us
    dot_general x4, matrix products, backward_step(): jnp.einsum('kgqs,qkgd->skd', prob_bf, grad_blk, preferred_element_type=jn...  16 us
    all_to_all x1, waiting for transfers between devices, body(): lax.all_to_all(grad_out, 'mp', split_axis=1, concat_axis=0, tiled=True)  14.1 us
    dot_general x4, matrix products, backward_step(): jnp.einsum('kgqs,skd->qkgd', grad_score, key_slab, preferred_element_type...  11.3 us
    another operation x1, loops' own time, body(): lax.scan(backward_step, (zeros, zeros), (block_ids,) + tuple(saved))  10.9 us
    another operation x1, loops' own time, body(): unused, saved = lax.scan(forward_step, jnp.int32(0), block_ids)  10.2 us
  transfers between devices with their start and end apart: 5, of which 5 were waited for; matrix products, arithmetic and copies ran while one was open for 2% of the time, Pallas kernels for 0%

commit v1 on v0

v1 whole, which is shorter than its diff:
```python
import math

import jax
import jax.numpy as jnp
from jax import lax
from jax.experimental import pallas as pl
from jax.experimental.pallas import tpu as pltpu
from jax.sharding import PartitionSpec as P

HEAD = 128
BLOCK = 128
WINDOW = 1024
CHIPS = 16
X = 4
SPAN = WINDOW + BLOCK
TILE = 384
ATTN_SCALE = 168.0 ** (-0.5)
EXP2_SCALE = ATTN_SCALE * math.log2(math.e)
NEG_FILL = -1e30
FAR = 1 << 20

MESH = pl.DeviceIdType.MESH
F32, BF16 = jnp.float32, jnp.bfloat16
NT = (((1,), (1,)), ((), ()))
NN = (((1,), (0,)), ((), ()))


def dot(a, b, dims):
    return lax.dot_general(a, b, dims, preferred_element_type=F32)


def unit(a, p, qs, gs, kx, vx, kt, vt, low, out, dq, dk, dv, s_scr, e_scr, d_scr):
    start = pl.multiple_of(p * BLOCK, BLOCK)
    q = qs[a, p]
    top = jnp.full((8, 2 * BLOCK), NEG_FILL, F32)
    row = lax.broadcasted_iota(jnp.int32, (BLOCK, 2 * BLOCK), 0)
    col = lax.broadcasted_iota(jnp.int32, (BLOCK, 2 * BLOCK), 1) % BLOCK
    for t in range(SPAN // TILE):
        s = dot(kx[a, pl.ds(start + t * TILE, TILE), :], q, NT)
        for u in range(TILE // BLOCK):
            tile = t * (TILE // BLOCK) + u
            ok = row >= low[tile, pl.ds(p, 1), :]
            if tile == WINDOW // BLOCK:
                ok = ok & (row <= col)
            part = jnp.where(ok, s[u * BLOCK : (u + 1) * BLOCK], NEG_FILL)
            s_scr[tile * BLOCK : (tile + 1) * BLOCK, :] = part
            top = jnp.maximum(top, jnp.max(part.reshape(BLOCK // 8, 8, 2 * BLOCK), axis=0))
    top = jnp.max(top, axis=0, keepdims=True)
    total = jnp.zeros((8, 2 * BLOCK), F32)
    for tile in range(SPAN // BLOCK):
        rows = slice(tile * BLOCK, (tile + 1) * BLOCK)
        e = jnp.exp2((s_scr[rows, :] - top) * EXP2_SCALE)
        total = total + jnp.sum(e.reshape(BLOCK // 8, 8, 2 * BLOCK), axis=0)
        e_scr[rows, :] = e.astype(BF16)
    inv = 1.0 / jnp.sum(total, axis=0, keepdims=True)
    window = pl.ds(start, SPAN)
    o_t = (dot(vt[a, :, window], e_scr[...], NN) * inv).astype(BF16)
    g_t = (gs[a, p].T.astype(F32) * inv).astype(BF16)
    delta = jnp.sum(g_t.astype(F32) * o_t.astype(F32), axis=0, keepdims=True)
    out[a, p] = o_t.T
    for t in range(SPAN // TILE):
        rows = slice(t * TILE, (t + 1) * TILE)
        key_rows = pl.ds(start + t * TILE, TILE)
        e = e_scr[rows, :]
        ds = (e.astype(F32) * (dot(vx[a, key_rows, :], g_t, NN) - delta)).astype(BF16)
        d_scr[rows, :] = ds
        dv[key_rows, :] += dot(e, g_t, NT)
        dk[key_rows, :] += dot(ds, q, NN)
    dq[a, p] = (dot(kt[a, :, window], d_scr[...], NN) * ATTN_SCALE).astype(BF16).T


def kernel(
    q_ref, k_ref, v_ref, g_ref, band_ref, seg_ref,
    attn_ref, dq_ref, dk_ref, dv_ref,
    qs, gs, kx, vx, kt, vt, low, out, dqs, dk, dv, s_scr, e_scr, d_scr,
    hk, hv, pk, pv, rk, rv, lk, lv,
    send, q_in, k_in, v_in, hk_in, hv_in, g_in, o_in, dq_in, rk_in, rv_in, lk_in, lv_in,
):
    me, x = lax.axis_index("ctx"), lax.axis_index("mp")
    chip, core = me // 2, me % 2
    after, before = lax.rem(chip + 1, CHIPS), lax.rem(chip + CHIPS - 1, CHIPS)
    mate = 2 * chip + 1 - core

    barrier = pltpu.get_barrier_semaphore()
    for step in range(1, 2 * X):
        peer = lax.rem(core * X + x + step, 2 * X)
        pl.semaphore_signal(
            barrier, inc=1, device_id=(2 * chip + peer // X, peer % X), device_id_type=MESH
        )
    for other in (after, before):
        for c in range(2):
            pl.semaphore_signal(barrier, inc=1, device_id=(2 * other + c, x), device_id_type=MESH)
    pl.semaphore_wait(barrier, 2 * X - 1 + 4)

    def push(src, dst, send_at, recv, to):
        pltpu.make_async_remote_copy(
            src_ref=src, dst_ref=dst, send_sem=send.at[send_at], recv_sem=recv,
            device_id=to, device_id_type=MESH,
        ).start()

    def wait(ref, sem):
        pltpu.make_async_copy(ref, ref, sem).wait()

    own_rows = pl.ds(pl.multiple_of(core * 512, 512), 512)
    local_rows = pl.ds(pl.multiple_of(WINDOW + core * 512, 512), 512)
    my_block = core * X + x

    def columns(head):
        return pl.ds(pl.multiple_of(head * HEAD, HEAD), HEAD)

    for a in range(2):
        for ref, buf, at, sem in ((k_ref, kx, 0, hk_in), (v_ref, vx, 1, hv_in)):
            for c in range(2):
                push(
                    ref.at[:, (2 * c + a) * HEAD : (2 * c + a + 1) * HEAD],
                    buf.at[a, own_rows, :], at, sem.at[a], (2 * after + c, x),
                )
        theirs, mine = 2 * (1 - core) + a, 2 * core + a
        for ref, buf, at, sem in ((k_ref, kx, 2, k_in), (v_ref, vx, 3, v_in)):
            push(ref.at[:, columns(theirs)], buf.at[a, local_rows, :], at, sem.at[a], (mate, x))
            pltpu.make_async_copy(ref.at[:, columns(mine)], buf.at[a, local_rows, :], sem.at[a]).start()
        for g in range(2):
            rows = slice(g * BLOCK, (g + 1) * BLOCK)
            dst = qs.at[a, pl.ds(core * X, X), rows, :]
            push(q_ref.at[:, :, columns(2 * theirs + g)], dst, 4, q_in.at[a], (mate, x))
            pltpu.make_async_copy(q_ref.at[:, :, columns(2 * mine + g)], dst, q_in.at[a]).start()
            dst = gs.at[a, my_block, rows, :]
            for step in range(1, 2 * X):
                peer = lax.rem(my_block + step, 2 * X)
                c, to_x = peer // X, peer % X
                push(
                    g_ref.at[:, columns(to_x * 8 + c * 4 + 2 * a + g)], dst, 5, g_in.at[a],
                    (2 * chip + c, to_x),
                )
            pltpu.make_async_copy(
                g_ref.at[:, columns(x * 8 + core * 4 + 2 * a + g)], dst, g_in.at[a]
            ).start()

    seg = seg_ref[pl.ds(pl.multiple_of(8 * chip, 8), 8), :]
    every = seg_ref[...]
    begin = jnp.zeros((8, BLOCK), jnp.int32)
    for s in range(1, 16):
        count = jnp.sum((every < s).astype(jnp.int32), axis=0, keepdims=True)
        count = jnp.sum(count, axis=1, keepdims=True)
        begin = jnp.maximum(begin, jnp.where(seg >= s, count, 0))
    block = lax.broadcasted_iota(jnp.int32, (8, BLOCK), 0)
    lane = lax.broadcasted_iota(jnp.int32, (8, BLOCK), 1)
    first = jnp.maximum(begin - (chip - 1) * WINDOW, block * BLOCK + lane + 1)
    bands = band_ref[pl.ds(pl.multiple_of(8 * chip, 8), 8), :]
    for tile in range(SPAN // BLOCK):
        o = WINDOW // BLOCK - tile
        value = first - (block + tile) * BLOCK + (1 - bands[:, o : o + 1]) * FAR
        low[tile] = jnp.concatenate([value, value], axis=1)

    def loop(i, carry):
        a, p = i // 8, i % 8

        @pl.when(p == 0)
        def _():
            wait(kx.at[a, WINDOW:, :], k_in.at[a])
            wait(vx.at[a, WINDOW:, :], v_in.at[a])
            wait(kx.at[a, :WINDOW, :], hk_in.at[a])
            wait(vx.at[a, :WINDOW, :], hv_in.at[a])

            def turn(b, c):
                rows = pl.ds(pl.multiple_of(b * BLOCK, BLOCK), BLOCK)
                kt[a, :, rows] = kx[a, rows, :].T
                vt[a, :, rows] = vx[a, rows, :].T
                return c

            lax.fori_loop(0, 16, turn, 0)
            dk[...] = jnp.zeros_like(dk)
            dv[...] = jnp.zeros_like(dv)
            wait(qs.at[a], q_in.at[a])
            wait(gs.at[a], g_in.at[a])

        unit(a, p, qs, gs, kx, vx, kt, vt, low, out, dqs, dk, dv, s_scr, e_scr, d_scr)

        head = 2 * core + a
        rows = pl.ds(pl.multiple_of(p * BLOCK, BLOCK), BLOCK)
        hk[a, p] = (dk[rows, :] * ATTN_SCALE).astype(BF16)
        hv[a, p] = dv[rows, :].astype(BF16)
        at_rows = pl.ds(pl.multiple_of((p % 4) * BLOCK, BLOCK), BLOCK)
        to = (2 * before + p // 4, x)
        push(hk.at[a, p], rk.at[head, at_rows, :], 6, rk_in.at[head], to)
        push(hv.at[a, p], rv.at[head, at_rows, :], 7, rv_in.at[head], to)
        for g in range(2):
            part = slice(g * BLOCK, (g + 1) * BLOCK)
            src = out.at[a, p, part, :]
            dst = attn_ref.at[:, columns(x * 8 + core * 4 + 2 * a + g)]

            @pl.when(p == my_block)
            def _():
                pltpu.make_async_copy(src, dst, o_in).start()

            @pl.when(p != my_block)
            def _():
                push(src, dst, 8, o_in, (2 * chip + p // 4, p % 4))

            src2 = dqs.at[a, p, part, :]
            dst2 = dq_ref.at[p % 4, :, columns(2 * head + g)]

            @pl.when(p // 4 == core)
            def _():
                pltpu.make_async_copy(src2, dst2, dq_in).start()

            @pl.when(p // 4 != core)
            def _():
                push(src2, dst2, 9, dq_in, (mate, x))

        @pl.when(p == 7)
        def _():
            theirs = pl.ds(pl.multiple_of(WINDOW + (1 - core) * 512, 512), 512)
            pk[a] = (dk[theirs, :] * ATTN_SCALE).astype(BF16)
            pv[a] = dv[theirs, :].astype(BF16)
            push(pk.at[a], lk.at[head], 10, lk_in.at[a], (mate, x))
            push(pv.at[a], lv.at[head], 11, lv_in.at[a], (mate, x))
            lk[head] = (dk[local_rows, :] * ATTN_SCALE).astype(BF16)
            lv[head] = dv[local_rows, :].astype(BF16)

        return carry

    lax.fori_loop(0, 16, loop, 0)

    for a in range(2):
        wait(lk.at[0], lk_in.at[a])
        wait(lv.at[0], lv_in.at[a])
    for h in range(4):
        cols = slice(h * HEAD, (h + 1) * HEAD)
        wait(rk.at[h], rk_in.at[h])
        wait(rv.at[h], rv_in.at[h])
        dk_ref[:, cols] = (lk[h].astype(F32) + rk[h].astype(F32)).astype(BF16)
        dv_ref[:, cols] = (lv[h].astype(F32) + rv[h].astype(F32)).astype(BF16)
    wait(attn_ref, o_in)
    wait(dq_ref, dq_in)
    wait(k_ref, send.at[0])
    wait(v_ref, send.at[1])
    wait(k_ref.at[:, : 2 * HEAD], send.at[2])
    wait(v_ref.at[:, : 2 * HEAD], send.at[3])
    wait(q_ref.at[:, :, : 4 * HEAD], send.at[4])
    wait(g_ref.at[:, : 28 * HEAD], send.at[5])
    wait(hk, send.at[6])
    wait(hv, send.at[7])
    wait(out.at[:, :7], send.at[8])
    wait(dqs.at[:, :4], send.at[9])
    wait(pk, send.at[10])
    wait(pv, send.at[11])


def body(queries, keys, values, grad_out, band_mask, segment_ids):
    hbm = pl.BlockSpec(memory_space=pl.ANY)
    vmem = pl.BlockSpec(memory_space=pltpu.VMEM)
    dma = pltpu.SemaphoreType.DMA
    attn, dq, dk, dv = pl.pallas_call(
        kernel,
        out_shape=(
            jax.ShapeDtypeStruct((128, 4096), BF16),
            jax.ShapeDtypeStruct((4, 128, 1024), BF16),
            jax.ShapeDtypeStruct((512, 512), BF16),
            jax.ShapeDtypeStruct((512, 512), BF16),
        ),
        in_specs=[hbm, hbm, hbm, hbm, vmem, vmem],
        out_specs=(hbm, hbm, vmem, vmem),
        scratch_shapes=[
            pltpu.VMEM((2, 8, 256, 128), BF16),
            pltpu.VMEM((2, 8, 256, 128), BF16),
            pltpu.VMEM((2, 2048, 128), BF16),
            pltpu.VMEM((2, 2048, 128), BF16),
            pltpu.VMEM((2, 128, 2048), BF16),
            pltpu.VMEM((2, 128, 2048), BF16),
            pltpu.VMEM((9, 8, 256), jnp.int32),
            pltpu.VMEM((2, 8, 256, 128), BF16),
            pltpu.VMEM((2, 8, 256, 128), BF16),
            pltpu.VMEM((2048, 128), F32),
            pltpu.VMEM((2048, 128), F32),
            pltpu.VMEM((SPAN, 256), F32),
            pltpu.VMEM((SPAN, 256), BF16),
            pltpu.VMEM((SPAN, 256), BF16),
            pltpu.VMEM((2, 8, 128, 128), BF16),
            pltpu.VMEM((2, 8, 128, 128), BF16),
            pltpu.VMEM((2, 512, 128), BF16),
            pltpu.VMEM((2, 512, 128), BF16),
            pltpu.VMEM((4, 512, 128), BF16),
            pltpu.VMEM((4, 512, 128), BF16),
            pltpu.VMEM((4, 512, 128), BF16),
            pltpu.VMEM((4, 512, 128), BF16),
            dma((12,)),
            dma((2,)), dma((2,)), dma((2,)), dma((2,)), dma((2,)), dma((2,)),
            dma(()), dma(()),
            dma((4,)), dma((4,)), dma((2,)), dma((2,)),
        ],
        compiler_params=pltpu.CompilerParams(
            collective_id=0, has_side_effects=True, vmem_limit_bytes=48 << 20
        ),
    )(queries.reshape(4, 128, 1024), keys, values, grad_out, band_mask, segment_ids.reshape(128, 128))
    return attn, dq.reshape(512, 1024), dk, dv


def solution(mesh):
    placed = (P("ctx", "mp"), P("ctx", "mp"), P("ctx", "mp"), P(("ctx", "mp"), None), P(), P())
    return jax.shard_map(
        body,
        mesh=mesh,
        in_specs=placed,
        out_specs=(P(("ctx", "mp"), None), P("ctx", "mp"), P("ctx", "mp"), P("ctx", "mp")),
        check_vma=False,
    )
```

time: 268 us -> 65.4 us (0.24)
  the two profiles are of different devices: /device:TPU:96 before, /device:TPU:1 now
where the time goes in v1:
time: 65.4 us; the launch traced here: 65.1 us
  Pallas kernels  56.8 us (87%)
  local copies, waits for them, and re-layouts  7.67 us (12%)
  between operations  0.66 us (1%)
    pallas_call x1, Pallas kernels, body(): pl.pallas_call(kernel, out_shape=(jax.ShapeDtypeStruct((128, 4096), BF16)...  56.8 us
    unnamed x13, local copies, waits for them, and re-layouts  7.67 us

profile of v1, /device:TPU:1, one launch (start us, length us, event | category | flops | bytes accessed | tf_op | source)
XLA Modules:
  0.0 65.1 jit_solution(7257435548467341462)
XLA Ops:
  0.6 0.0 copy-start.3
  0.6 0.8 %copy.10.band_ref = s32[128,9]{1,0:T(8,128)S(1)} copy(s32[128,9]{0,1:T(8,128)} %param.10) | data formatting | bytes 9216 | tf_op args[4]
  1.5 0.0 copy-done.3
  1.5 0.0 copy-start
  1.5 1.2 %copy-done = bf16[512,1024]{1,0:T(8,128)(2,1)S(1)} copy-done((bf16[512,1024]{1,0:T(8,128)(2,1)S(1)}, bf16[512,1024]{1,0:T(8,128)(2,1)}, u32[]{:S(2)}) %copy-start) | copy-done | bytes 1048600
  2.7 0.0 copy-start.1
  2.7 1.0 %copy-done.1 = bf16[512,512]{1,0:T(8,128)(2,1)S(1)} copy-done((bf16[512,512]{1,0:T(8,128)(2,1)S(1)}, bf16[512,512]{1,0:T(8,128)(2,1)}, u32[]{:S(2)}) %copy-start.1) | copy-done | bytes 524312
  3.7 0.0 copy-start.2
  3.8 1.0 %copy-done.2 = bf16[512,512]{1,0:T(8,128)(2,1)S(1)} copy-done((bf16[512,512]{1,0:T(8,128)(2,1)S(1)}, bf16[512,512]{1,0:T(8,128)(2,1)}, u32[]{:S(2)}) %copy-start.2) | copy-done | bytes 524312
  4.8 56.8 %shard_map.93 = (bf16[128,4096]{1,0:T(8,128)(2,1)S(1)}, bf16[4,128,1024]{2,1,0:T(8,128)(2,1)S(1)}, bf16[512,512]{1,0:T(8,128)(2,1)S(1)}, bf16[512,512]{1,0:T(8,128)(2,1)S(1)}) custom-call(bf16[4,128,1024]{2,1,0:T(8,128)(2,1)S(1)} %bitcast.3, bf16[512,512]{1,0:T(8,128)(2,1)S(1)} %copy-done.1, bf16[512,512]{1,0:T(8,128)(2,1)S(1)} %copy-done.2, ...), custom_call_target="tpu_custom_call" | custom-call | tf_op jit(solution)/shard_map/pallas_call | solution.py:254
  61.6 1.0 %copy.15 = bf16[128,4096]{1,0:T(8,128)(2,1)} copy(bf16[128,4096]{1,0:T(8,128)(2,1)S(1)} %get-tuple-element.16) | data formatting | bytes 2097152
  62.6 1.0 %copy.16 = bf16[512,1024]{1,0:T(8,128)(2,1)} copy(bf16[512,1024]{1,0:T(8,128)(2,1)S(1)} %bitcast.4) | data formatting | bytes 2097152
  63.5 0.8 %copy.17 = bf16[512,512]{1,0:T(8,128)(2,1)} copy(bf16[512,512]{1,0:T(8,128)(2,1)S(1)} %get-tuple-element.18) | data formatting | bytes 1048576
  64.3 0.8 %copy.18 = bf16[512,512]{1,0:T(8,128)(2,1)} copy(bf16[512,512]{1,0:T(8,128)(2,1)S(1)} %get-tuple-element.19) | data formatting | bytes 1048576
Async XLA Ops:
  0.6 0.8 %copy-start.3 = (s32[16384]{0:T(1024)S(1)}, s32[16384]{0:T(1024)}, u32[]{:S(2)}) copy-start(s32[16384]{0:T(1024)} %param.11) | copy-start | bytes 196612
  1.5 1.2 %copy-start = (bf16[512,1024]{1,0:T(8,128)(2,1)S(1)}, bf16[512,1024]{1,0:T(8,128)(2,1)}, u32[]{:S(2)}) copy-start(bf16[512,1024]{1,0:T(8,128)(2,1)} %param.6) | copy-start | bytes 3145732
  2.7 1.0 %copy-start.1 = (bf16[512,512]{1,0:T(8,128)(2,1)S(1)}, bf16[512,512]{1,0:T(8,128)(2,1)}, u32[]{:S(2)}) copy-start(bf16[512,512]{1,0:T(8,128)(2,1)} %k_ref.1) | copy-start | bytes 1572868
  3.7 1.0 %copy-start.2 = (bf16[512,512]{1,0:T(8,128)(2,1)S(1)}, bf16[512,512]{1,0:T(8,128)(2,1)}, u32[]{:S(2)}) copy-start(bf16[512,512]{1,0:T(8,128)(2,1)} %v_ref.1) | copy-start | bytes 1572868

commit v2 on v1

--- a/solution.py
+++ b/solution.py
@@ -29,7 +29,7 @@
     return lax.dot_general(a, b, dims, preferred_element_type=F32)
 
 
-def unit(a, p, qs, gs, kx, vx, kt, vt, low, out, dq, dk, dv, s_scr, e_scr, d_scr):
+def scores(a, p, qs, kx, low, s_scr, e_scr, inv_scr):
     start = pl.multiple_of(p * BLOCK, BLOCK)
     q = qs[a, p]
     top = jnp.full((8, 2 * BLOCK), NEG_FILL, F32)
@@ -45,6 +45,7 @@
             part = jnp.where(ok, s[u * BLOCK : (u + 1) * BLOCK], NEG_FILL)
             s_scr[tile * BLOCK : (tile + 1) * BLOCK, :] = part
             top = jnp.maximum(top, jnp.max(part.reshape(BLOCK // 8, 8, 2 * BLOCK), axis=0))
+        yield
     top = jnp.max(top, axis=0, keepdims=True)
     total = jnp.zeros((8, 2 * BLOCK), F32)
     for tile in range(SPAN // BLOCK):
@@ -52,29 +53,49 @@
         e = jnp.exp2((s_scr[rows, :] - top) * EXP2_SCALE)
         total = total + jnp.sum(e.reshape(BLOCK // 8, 8, 2 * BLOCK), axis=0)
         e_scr[rows, :] = e.astype(BF16)
+        yield
     inv = 1.0 / jnp.sum(total, axis=0, keepdims=True)
+    inv_scr[...] = jnp.broadcast_to(inv, (8, 2 * BLOCK))
+
+
+def gradients(a, p, qs, gs, kx, vx, kt, vt, out, dq, dk, dv, e_scr, inv_scr, d_scr):
+    start = pl.multiple_of(p * BLOCK, BLOCK)
     window = pl.ds(start, SPAN)
+    q = qs[a, p]
+    inv = inv_scr[0:1, :]
+    g_t = (gs[a, p].T.astype(F32) * inv).astype(BF16)
     o_t = (dot(vt[a, :, window], e_scr[...], NN) * inv).astype(BF16)
-    g_t = (gs[a, p].T.astype(F32) * inv).astype(BF16)
     delta = jnp.sum(g_t.astype(F32) * o_t.astype(F32), axis=0, keepdims=True)
     out[a, p] = o_t.T
+    yield
     for t in range(SPAN // TILE):
         rows = slice(t * TILE, (t + 1) * TILE)
         key_rows = pl.ds(start + t * TILE, TILE)
         e = e_scr[rows, :]
         ds = (e.astype(F32) * (dot(vx[a, key_rows, :], g_t, NN) - delta)).astype(BF16)
         d_scr[rows, :] = ds
-        dv[key_rows, :] += dot(e, g_t, NT)
-        dk[key_rows, :] += dot(ds, q, NN)
+        yield
+        dv[a, key_rows, :] += dot(e, g_t, NT)
+        dk[a, key_rows, :] += dot(ds, q, NN)
+        yield
     dq[a, p] = (dot(kt[a, :, window], d_scr[...], NN) * ATTN_SCALE).astype(BF16).T
+
+
+def interleave(first, second):
+    live = True
+    while live:
+        live = False
+        for chunks, times in ((first, 1), (second, 3)):
+            for _ in range(times):
+                live = next(chunks, chunks) is not chunks or live
 
 
 def kernel(
     q_ref, k_ref, v_ref, g_ref, band_ref, seg_ref,
-    attn_ref, dq_ref, dk_ref, dv_ref,
-    qs, gs, kx, vx, kt, vt, low, out, dqs, dk, dv, s_scr, e_scr, d_scr,
-    hk, hv, pk, pv, rk, rv, lk, lv,
-    send, q_in, k_in, v_in, hk_in, hv_in, g_in, o_in, dq_in, rk_in, rv_in, lk_in, lv_in,
+    attn_ref, dq_ref, lk, lv, rk, rv,
+    qs, gs, kx, vx, kt, vt, low, out, dqs, dk, dv, s_scr, e_0, e_1, inv_0, inv_1, d_scr,
+    hk, hv, pk, pv, seg_v, band_v, band_t,
+    send, q_in, k_in, v_in, hk_in, hv_in, g_in, o_in, dq_in, rk_in, rv_in, lk_in, lv_in, seg_in, band_in,
 ):
     me, x = lax.axis_index("ctx"), lax.axis_index("mp")
     chip, core = me // 2, me % 2
@@ -90,7 +111,6 @@
     for other in (after, before):
         for c in range(2):
             pl.semaphore_signal(barrier, inc=1, device_id=(2 * other + c, x), device_id_type=MESH)
-    pl.semaphore_wait(barrier, 2 * X - 1 + 4)
 
     def push(src, dst, send_at, recv, to):
         pltpu.make_async_remote_copy(
@@ -107,6 +127,10 @@
 
     def columns(head):
         return pl.ds(pl.multiple_of(head * HEAD, HEAD), HEAD)
+
+    pltpu.make_async_copy(seg_ref, seg_v, seg_in).start()
+    pltpu.make_async_copy(band_ref, band_v, band_in).start()
+    pl.semaphore_wait(barrier, 2 * X - 1 + 4)
 
     for a in range(2):
         for ref, buf, at, sem in ((k_ref, kx, 0, hk_in), (v_ref, vx, 1, hv_in)):
@@ -125,19 +149,25 @@
             push(q_ref.at[:, :, columns(2 * theirs + g)], dst, 4, q_in.at[a], (mate, x))
             pltpu.make_async_copy(q_ref.at[:, :, columns(2 * mine + g)], dst, q_in.at[a]).start()
             dst = gs.at[a, my_block, rows, :]
-            for step in range(1, 2 * X):
+            pltpu.make_async_copy(
+                g_ref.at[:, columns(x * 8 + core * 4 + 2 * a + g)], dst, g_in.at[a]
+            ).start()
+
+            def spread(step, carry, dst=dst, a=a, g=g):
                 peer = lax.rem(my_block + step, 2 * X)
                 c, to_x = peer // X, peer % X
                 push(
                     g_ref.at[:, columns(to_x * 8 + c * 4 + 2 * a + g)], dst, 5, g_in.at[a],
                     (2 * chip + c, to_x),
                 )
-            pltpu.make_async_copy(
-                g_ref.at[:, columns(x * 8 + core * 4 + 2 * a + g)], dst, g_in.at[a]
-            ).start()
-
-    seg = seg_ref[pl.ds(pl.multiple_of(8 * chip, 8), 8), :]
-    every = seg_ref[...]
+                return carry
+
+            lax.fori_loop(1, 2 * X, spread, 0)
+
+    wait(seg_v, seg_in)
+    wait(band_v, band_in)
+    seg = seg_v[pl.ds(pl.multiple_of(8 * chip, 8), 8), :]
+    every = seg_v[...]
     begin = jnp.zeros((8, BLOCK), jnp.int32)
     for s in range(1, 16):
         count = jnp.sum((every < s).astype(jnp.int32), axis=0, keepdims=True)
@@ -146,40 +176,55 @@
     block = lax.broadcasted_iota(jnp.int32, (8, BLOCK), 0)
     lane = lax.broadcasted_iota(jnp.int32, (8, BLOCK), 1)
     first = jnp.maximum(begin - (chip - 1) * WINDOW, block * BLOCK + lane + 1)
-    bands = band_ref[pl.ds(pl.multiple_of(8 * chip, 8), 8), :]
+    bands = jnp.concatenate([band_v[...], jnp.zeros((7, 128), jnp.int32)], axis=0)
+    band_t[...] = bands.T
+    bands = band_t[pl.ds(pl.multiple_of(8 * chip, 8), 8), :]
     for tile in range(SPAN // BLOCK):
         o = WINDOW // BLOCK - tile
         value = first - (block + tile) * BLOCK + (1 - bands[:, o : o + 1]) * FAR
         low[tile] = jnp.concatenate([value, value], axis=1)
 
-    def loop(i, carry):
+    def turn(a, b):
+        rows = pl.ds(pl.multiple_of(b * BLOCK, BLOCK), BLOCK)
+        kt[a, :, rows] = kx[a, rows, :].T
+        vt[a, :, rows] = vx[a, rows, :].T
+
+    def turn_local(i, carry):
+        turn(i // 8, 8 + i % 8)
+        return carry
+
+    def turn_halo(i, carry):
+        turn(carry, i)
+        return carry
+
+    def score_inputs(a):
+        wait(kx.at[a, :WINDOW, :], hk_in.at[a])
+        wait(vx.at[a, :WINDOW, :], hv_in.at[a])
+        lax.fori_loop(0, 8, turn_halo, a)
+
+    dk[...] = jnp.zeros_like(dk)
+    dv[...] = jnp.zeros_like(dv)
+    for a in range(2):
+        wait(kx.at[a, WINDOW:, :], k_in.at[a])
+        wait(vx.at[a, WINDOW:, :], v_in.at[a])
+        wait(qs.at[a], q_in.at[a])
+    lax.fori_loop(0, 16, turn_local, 0)
+    e_scr, inv_scr = (e_0, e_1), (inv_0, inv_1)
+
+    def score(i, slot):
+        return scores(i // 8, i % 8, qs, kx, low, s_scr, e_scr[slot], inv_scr[slot])
+
+    def grad(i, slot):
+        return gradients(
+            i // 8, i % 8, qs, gs, kx, vx, kt, vt, out, dqs, dk, dv, e_scr[slot], inv_scr[slot], d_scr
+        )
+
+    def deliver(i):
         a, p = i // 8, i % 8
-
-        @pl.when(p == 0)
-        def _():
-            wait(kx.at[a, WINDOW:, :], k_in.at[a])
-            wait(vx.at[a, WINDOW:, :], v_in.at[a])
-            wait(kx.at[a, :WINDOW, :], hk_in.at[a])
-            wait(vx.at[a, :WINDOW, :], hv_in.at[a])
-
-            def turn(b, c):
-                rows = pl.ds(pl.multiple_of(b * BLOCK, BLOCK), BLOCK)
-                kt[a, :, rows] = kx[a, rows, :].T
-                vt[a, :, rows] = vx[a, rows, :].T
-                return c
-
-            lax.fori_loop(0, 16, turn, 0)
-            dk[...] = jnp.zeros_like(dk)
-            dv[...] = jnp.zeros_like(dv)
-            wait(qs.at[a], q_in.at[a])
-            wait(gs.at[a], g_in.at[a])
-
-        unit(a, p, qs, gs, kx, vx, kt, vt, low, out, dqs, dk, dv, s_scr, e_scr, d_scr)
-
         head = 2 * core + a
         rows = pl.ds(pl.multiple_of(p * BLOCK, BLOCK), BLOCK)
-        hk[a, p] = (dk[rows, :] * ATTN_SCALE).astype(BF16)
-        hv[a, p] = dv[rows, :].astype(BF16)
+        hk[a, p] = (dk[a, rows, :] * ATTN_SCALE).astype(BF16)
+        hv[a, p] = dv[a, rows, :].astype(BF16)
         at_rows = pl.ds(pl.multiple_of((p % 4) * BLOCK, BLOCK), BLOCK)
         to = (2 * before + p // 4, x)
         push(hk.at[a, p], rk.at[head, at_rows, :], 6, rk_in.at[head], to)
@@ -211,26 +256,39 @@
         @pl.when(p == 7)
         def _():
             theirs = pl.ds(pl.multiple_of(WINDOW + (1 - core) * 512, 512), 512)
-            pk[a] = (dk[theirs, :] * ATTN_SCALE).astype(BF16)
-            pv[a] = dv[theirs, :].astype(BF16)
+            pk[a] = (dk[a, theirs, :] * ATTN_SCALE).astype(BF16)
+            pv[a] = dv[a, theirs, :].astype(BF16)
             push(pk.at[a], lk.at[head], 10, lk_in.at[a], (mate, x))
             push(pv.at[a], lv.at[head], 11, lv_in.at[a], (mate, x))
-            lk[head] = (dk[local_rows, :] * ATTN_SCALE).astype(BF16)
-            lv[head] = dv[local_rows, :].astype(BF16)
-
+            lk[head] = (dk[a, local_rows, :] * ATTN_SCALE).astype(BF16)
+            lv[head] = dv[a, local_rows, :].astype(BF16)
+
+    score_inputs(0)
+    for _ in score(0, 0):
+        pass
+    wait(gs.at[0], g_in.at[0])
+
+    def loop(j, carry):
+        interleave(grad(2 * j, 0), score(2 * j + 1, 1))
+        deliver(2 * j)
+
+        @pl.when(j == 3)
+        def _():
+            score_inputs(1)
+            wait(gs.at[1], g_in.at[1])
+
+        interleave(grad(2 * j + 1, 1), score(jnp.minimum(2 * j + 2, 15), 0))
+        deliver(2 * j + 1)
         return carry
 
-    lax.fori_loop(0, 16, loop, 0)
+    lax.fori_loop(0, 8, loop, 0)
 
     for a in range(2):
         wait(lk.at[0], lk_in.at[a])
         wait(lv.at[0], lv_in.at[a])
     for h in range(4):
-        cols = slice(h * HEAD, (h + 1) * HEAD)
         wait(rk.at[h], rk_in.at[h])
         wait(rv.at[h], rv_in.at[h])
-        dk_ref[:, cols] = (lk[h].astype(F32) + rk[h].astype(F32)).astype(BF16)
-        dv_ref[:, cols] = (lv[h].astype(F32) + rv[h].astype(F32)).astype(BF16)
     wait(attn_ref, o_in)
     wait(dq_ref, dq_in)
     wait(k_ref, send.at[0])
@@ -247,20 +305,37 @@
     wait(pv, send.at[11])
 
 
+def finish(attn_ref, dq_ref, lk, lv, rk, rv, attn_out, dq_out, dk_out, dv_out, dk, dv, sems):
+    copies = [
+        pltpu.make_async_copy(attn_ref, attn_out, sems.at[0]),
+        pltpu.make_async_copy(dq_ref, dq_out, sems.at[1]),
+        pltpu.make_async_copy(dk, dk_out, sems.at[2]),
+        pltpu.make_async_copy(dv, dv_out, sems.at[3]),
+    ]
+    copies[0].start()
+    copies[1].start()
+    for ours, other, total, copy in ((lk, rk, dk, copies[2]), (lv, rv, dv, copies[3])):
+        for h in range(4):
+            cols = slice(h * HEAD, (h + 1) * HEAD)
+            total[:, cols] = (ours[h].astype(F32) + other[h].astype(F32)).astype(BF16)
+        copy.start()
+    for copy in copies:
+        copy.wait()
+
+
 def body(queries, keys, values, grad_out, band_mask, segment_ids):
-    hbm = pl.BlockSpec(memory_space=pl.ANY)
+    hbm = pl.BlockSpec(memory_space=pltpu.HBM)
+    anywhere = pl.BlockSpec(memory_space=pl.ANY)
     vmem = pl.BlockSpec(memory_space=pltpu.VMEM)
     dma = pltpu.SemaphoreType.DMA
-    attn, dq, dk, dv = pl.pallas_call(
+    attn_shape = jax.ShapeDtypeStruct((128, 4096), BF16)
+    dq_shape = jax.ShapeDtypeStruct((4, 128, 1024), BF16)
+    part = jax.ShapeDtypeStruct((4, 512, 128), BF16)
+    pieces = pl.pallas_call(
         kernel,
-        out_shape=(
-            jax.ShapeDtypeStruct((128, 4096), BF16),
-            jax.ShapeDtypeStruct((4, 128, 1024), BF16),
-            jax.ShapeDtypeStruct((512, 512), BF16),
-            jax.ShapeDtypeStruct((512, 512), BF16),
-        ),
-        in_specs=[hbm, hbm, hbm, hbm, vmem, vmem],
-        out_specs=(hbm, hbm, vmem, vmem),
+        out_shape=(attn_shape, dq_shape, part, part, part, part),
+        in_specs=[hbm] * 6,
+        out_specs=(anywhere, anywhere, vmem, vmem, vmem, vmem),
         scratch_shapes=[
             pltpu.VMEM((2, 8, 256, 128), BF16),
             pltpu.VMEM((2, 8, 256, 128), BF16),
@@ -271,28 +346,48 @@
             pltpu.VMEM((9, 8, 256), jnp.int32),
             pltpu.VMEM((2, 8, 256, 128), BF16),
             pltpu.VMEM((2, 8, 256, 128), BF16),
-            pltpu.VMEM((2048, 128), F32),
-            pltpu.VMEM((2048, 128), F32),
+            pltpu.VMEM((2, 2048, 128), F32),
+            pltpu.VMEM((2, 2048, 128), F32),
             pltpu.VMEM((SPAN, 256), F32),
             pltpu.VMEM((SPAN, 256), BF16),
+            pltpu.VMEM((SPAN, 256), BF16),
+            pltpu.VMEM((8, 256), F32),
+            pltpu.VMEM((8, 256), F32),
             pltpu.VMEM((SPAN, 256), BF16),
             pltpu.VMEM((2, 8, 128, 128), BF16),
             pltpu.VMEM((2, 8, 128, 128), BF16),
             pltpu.VMEM((2, 512, 128), BF16),
             pltpu.VMEM((2, 512, 128), BF16),
-            pltpu.VMEM((4, 512, 128), BF16),
-            pltpu.VMEM((4, 512, 128), BF16),
-            pltpu.VMEM((4, 512, 128), BF16),
-            pltpu.VMEM((4, 512, 128), BF16),
+            pltpu.VMEM((128, 128), jnp.int32),
+            pltpu.VMEM((9, 128), jnp.int32),
+            pltpu.VMEM((128, 16), jnp.int32),
             dma((12,)),
             dma((2,)), dma((2,)), dma((2,)), dma((2,)), dma((2,)), dma((2,)),
             dma(()), dma(()),
             dma((4,)), dma((4,)), dma((2,)), dma((2,)),
+            dma(()), dma(()),
         ],
         compiler_params=pltpu.CompilerParams(
             collective_id=0, has_side_effects=True, vmem_limit_bytes=48 << 20
         ),
-    )(queries.reshape(4, 128, 1024), keys, values, grad_out, band_mask, segment_ids.reshape(128, 128))
+    )(
+        *(
+            pltpu.with_memory_space_constraint(array, pltpu.HBM)
+            for array in (
+                queries.reshape(4, 128, 1024), keys, values, grad_out,
+                band_mask.T, segment_ids.reshape(128, 128),
+            )
+        )
+    )
+    grad = jax.ShapeDtypeStruct((512, 512), BF16)
+    attn, dq, dk, dv = pl.pallas_call(
+        finish,
+        out_shape=(attn_shape, dq_shape, grad, grad),
+        in_specs=[anywhere, anywhere, vmem, vmem, vmem, vmem],
+        out_specs=(hbm,) * 4,
+        scratch_shapes=[pltpu.VMEM((512, 512), BF16), pltpu.VMEM((512, 512), BF16), dma((4,))],
+        compiler_params=pltpu.CompilerParams(vmem_limit_bytes=16 << 20),
+    )(*pieces)
     return attn, dq.reshape(512, 1024), dk, dv
 
 

time: 65.4 us -> 53.3 us (0.81)
  local copies, waits for them, and re-layouts: 7.67 us -> 0 us
  Pallas kernels: 56.8 us -> 52.6 us
    unnamed x13 -> x0, local copies, waits for them, and re-layouts: 7.67 us -> none
    pallas_call x1 -> x2, Pallas kernels: 56.8 us -> 52.6 us  [the longest x1 50.9 us: body(): pl.pallas_call(kernel, out_shape=(attn_shape, dq_shape, part, part, part,...]
where the time goes in v2:
time: 53.3 us; the launch traced here: 53.2 us
  Pallas kernels  52.6 us (99%)
  between operations  0.64 us (1%)
    pallas_call x1, Pallas kernels, body(): pl.pallas_call(kernel, out_shape=(attn_shape, dq_shape, part, part, part,...  50.9 us
    pallas_call x1, Pallas kernels, body(): pl.pallas_call(finish, out_shape=(attn_shape, dq_shape, grad, grad), in_s...  1.69 us

profile of v2, /device:TPU:1, one launch (start us, length us, event | category | flops | bytes accessed | tf_op | source)
XLA Modules:
  0.0 53.2 jit_solution(41679536162871404)
XLA Ops:
  0.6 50.9 %shard_map.93 = (bf16[128,4096]{1,0:T(8,128)(2,1)S(1)}, bf16[4,128,1024]{2,1,0:T(8,128)(2,1)S(1)}, bf16[4,512,128]{2,1,0:T(8,128)(2,1)S(1)}, bf16[4,512,128]{2,1...) custom-call(bf16[4,128,1024]{2,1,0:T(8,128)(2,1)} %bitcast.4, ...), custom_call_target="tpu_custom_call" | custom-call | tf_op jit(solution)/shard_map/pallas_call | solution.py:334
  51.5 1.7 %shard_map.94 = (bf16[128,4096]{1,0:T(8,128)(2,1)}, bf16[4,128,1024]{2,1,0:T(8,128)(2,1)}, bf16[512,512]{1,0:T(8,128)(2,1)}, bf16[512,512]{1,0:T(8,128)(2,1)}) custom-call(bf16[128,4096]{1,0:T(8,128)(2,1)S(1)} %get-tuple-element.14.attn_ref, bf16[4,128,1024]{2,1,0:T(8,128)(2,1)S(1)} %get-tuple-element.15.dq_ref, ...), custom_call_target="tpu_custom_call" | custom-call | tf_op jit(solution)/shard_map/pallas_call | solution.py:383

commit v3 on v2

--- a/solution.py
+++ b/solution.py
@@ -17,6 +17,7 @@
 ATTN_SCALE = 168.0 ** (-0.5)
 EXP2_SCALE = ATTN_SCALE * math.log2(math.e)
 NEG_FILL = -1e30
+ORDER = ((0, 1), (1, 0))
 FAR = 1 << 20
 
 MESH = pl.DeviceIdType.MESH
@@ -100,6 +101,7 @@
     me, x = lax.axis_index("ctx"), lax.axis_index("mp")
     chip, core = me // 2, me % 2
     after, before = lax.rem(chip + 1, CHIPS), lax.rem(chip + CHIPS - 1, CHIPS)
+    has_after, has_before = chip < CHIPS - 1, chip > 0
     mate = 2 * chip + 1 - core
 
     barrier = pltpu.get_barrier_semaphore()
@@ -108,9 +110,15 @@
         pl.semaphore_signal(
             barrier, inc=1, device_id=(2 * chip + peer // X, peer % X), device_id_type=MESH
         )
-    for other in (after, before):
-        for c in range(2):
-            pl.semaphore_signal(barrier, inc=1, device_id=(2 * other + c, x), device_id_type=MESH)
+    for other, there in ((after, has_after), (before, has_before)):
+
+        @pl.when(there)
+        def _(other=other):
+            for c in range(2):
+                pl.semaphore_signal(
+                    barrier, inc=1, device_id=(2 * other + c, x), device_id_type=MESH
+                )
+
 
     def push(src, dst, send_at, recv, to):
         pltpu.make_async_remote_copy(
@@ -121,7 +129,6 @@
     def wait(ref, sem):
         pltpu.make_async_copy(ref, ref, sem).wait()
 
-    own_rows = pl.ds(pl.multiple_of(core * 512, 512), 512)
     local_rows = pl.ds(pl.multiple_of(WINDOW + core * 512, 512), 512)
     my_block = core * X + x
 
@@ -130,15 +137,23 @@
 
     pltpu.make_async_copy(seg_ref, seg_v, seg_in).start()
     pltpu.make_async_copy(band_ref, band_v, band_in).start()
-    pl.semaphore_wait(barrier, 2 * X - 1 + 4)
+    neighbours = jnp.minimum(chip, 1) + jnp.minimum(CHIPS - 1 - chip, 1)
+    pl.semaphore_wait(barrier, 2 * X - 1 + 2 * neighbours)
 
     for a in range(2):
-        for ref, buf, at, sem in ((k_ref, kx, 0, hk_in), (v_ref, vx, 1, hv_in)):
-            for c in range(2):
-                push(
-                    ref.at[:, (2 * c + a) * HEAD : (2 * c + a + 1) * HEAD],
-                    buf.at[a, own_rows, :], at, sem.at[a], (2 * after + c, x),
-                )
+
+        @pl.when(has_after)
+        def _(a=a):
+            for c in ORDER[a]:
+                for b in range(3, -1, -1):
+                    rows = slice(b * BLOCK, (b + 1) * BLOCK)
+                    to_rows = pl.ds(pl.multiple_of(core * 512 + b * BLOCK, BLOCK), BLOCK)
+                    for ref, buf, at, sem in ((k_ref, kx, 0, hk_in), (v_ref, vx, 1, hv_in)):
+                        push(
+                            ref.at[rows, (2 * c + a) * HEAD : (2 * c + a + 1) * HEAD],
+                            buf.at[a, to_rows, :], at, sem.at[a, 4 * core + b], (2 * after + c, x),
+                        )
+
         theirs, mine = 2 * (1 - core) + a, 2 * core + a
         for ref, buf, at, sem in ((k_ref, kx, 2, k_in), (v_ref, vx, 3, v_in)):
             push(ref.at[:, columns(theirs)], buf.at[a, local_rows, :], at, sem.at[a], (mate, x))
@@ -193,14 +208,45 @@
         turn(i // 8, 8 + i % 8)
         return carry
 
-    def turn_halo(i, carry):
-        turn(carry, i)
-        return carry
-
-    def score_inputs(a):
-        wait(kx.at[a, :WINDOW, :], hk_in.at[a])
-        wait(vx.at[a, :WINDOW, :], hv_in.at[a])
-        lax.fori_loop(0, 8, turn_halo, a)
+    def block_of(i):
+        r = i % 8
+        return (r + 5) % 8 + (2 - 2 * r) * (1 - (r + 5) // 8)
+
+    def take_halo(a, b):
+        rows = pl.ds(pl.multiple_of(b * BLOCK, BLOCK), BLOCK)
+
+        @pl.when(has_before)
+        def _():
+            wait(kx.at[a, rows, :], hk_in.at[a, b])
+            wait(vx.at[a, rows, :], hv_in.at[a, b])
+
+        turn(a, b)
+
+    def score_inputs(i):
+        a, r = i // 8, i % 8
+
+        @pl.when(r < 3)
+        def _():
+            take_halo(a, 7 - r)
+
+        @pl.when(r == 3)
+        def _():
+            def step(b, carry):
+                take_halo(a, 4 - b)
+                return carry
+
+            lax.fori_loop(0, 5, step, 0)
+
+    @pl.when(chip == 0)
+    def _():
+        for a in range(2):
+            kx[a, :WINDOW, :] = jnp.zeros((WINDOW, HEAD), BF16)
+            vx[a, :WINDOW, :] = jnp.zeros((WINDOW, HEAD), BF16)
+
+    @pl.when(chip == CHIPS - 1)
+    def _():
+        rk[...] = jnp.zeros_like(rk)
+        rv[...] = jnp.zeros_like(rv)
 
     dk[...] = jnp.zeros_like(dk)
     dv[...] = jnp.zeros_like(dv)
@@ -212,23 +258,35 @@
     e_scr, inv_scr = (e_0, e_1), (inv_0, inv_1)
 
     def score(i, slot):
-        return scores(i // 8, i % 8, qs, kx, low, s_scr, e_scr[slot], inv_scr[slot])
+        return scores(i // 8, block_of(i), qs, kx, low, s_scr, e_scr[slot], inv_scr[slot])
 
     def grad(i, slot):
         return gradients(
-            i // 8, i % 8, qs, gs, kx, vx, kt, vt, out, dqs, dk, dv, e_scr[slot], inv_scr[slot], d_scr
+            i // 8, block_of(i), qs, gs, kx, vx, kt, vt, out, dqs, dk, dv, e_scr[slot], inv_scr[slot], d_scr
         )
 
     def deliver(i):
-        a, p = i // 8, i % 8
+        a, r, p = i // 8, i % 8, block_of(i)
         head = 2 * core + a
-        rows = pl.ds(pl.multiple_of(p * BLOCK, BLOCK), BLOCK)
-        hk[a, p] = (dk[a, rows, :] * ATTN_SCALE).astype(BF16)
-        hv[a, p] = dv[a, rows, :].astype(BF16)
-        at_rows = pl.ds(pl.multiple_of((p % 4) * BLOCK, BLOCK), BLOCK)
-        to = (2 * before + p // 4, x)
-        push(hk.at[a, p], rk.at[head, at_rows, :], 6, rk_in.at[head], to)
-        push(hv.at[a, p], rv.at[head, at_rows, :], 7, rv_in.at[head], to)
+
+        def give(b, carry):
+            rows = pl.ds(pl.multiple_of(b * BLOCK, BLOCK), BLOCK)
+            hk[a, b] = (dk[a, rows, :] * ATTN_SCALE).astype(BF16)
+            hv[a, b] = dv[a, rows, :].astype(BF16)
+            at_rows = pl.ds(pl.multiple_of((b % 4) * BLOCK, BLOCK), BLOCK)
+            to = (2 * before + b // 4, x)
+            push(hk.at[a, b], rk.at[head, at_rows, :], 6, rk_in.at[head], to)
+            push(hv.at[a, b], rv.at[head, at_rows, :], 7, rv_in.at[head], to)
+            return carry
+
+        @pl.when(has_before & (r >= 3))
+        def _():
+            give(p, 0)
+
+        @pl.when(has_before & (r == 7))
+        def _():
+            lax.fori_loop(5, 8, give, 0)
+
         for g in range(2):
             part = slice(g * BLOCK, (g + 1) * BLOCK)
             src = out.at[a, p, part, :]
@@ -253,7 +311,7 @@
             def _():
                 push(src2, dst2, 9, dq_in, (mate, x))
 
-        @pl.when(p == 7)
+        @pl.when(r == 7)
         def _():
             theirs = pl.ds(pl.multiple_of(WINDOW + (1 - core) * 512, 512), 512)
             pk[a] = (dk[a, theirs, :] * ATTN_SCALE).astype(BF16)
@@ -263,19 +321,23 @@
             lk[head] = (dk[a, local_rows, :] * ATTN_SCALE).astype(BF16)
             lv[head] = dv[a, local_rows, :].astype(BF16)
 
-    score_inputs(0)
-    for _ in score(0, 0):
+    score_inputs(jnp.int32(0))
+    for _ in score(jnp.int32(0), 0):
         pass
     wait(gs.at[0], g_in.at[0])
 
     def loop(j, carry):
+        score_inputs(2 * j + 1)
         interleave(grad(2 * j, 0), score(2 * j + 1, 1))
         deliver(2 * j)
 
         @pl.when(j == 3)
         def _():
-            score_inputs(1)
             wait(gs.at[1], g_in.at[1])
+
+        @pl.when(j < 7)
+        def _():
+            score_inputs(2 * j + 2)
 
         interleave(grad(2 * j + 1, 1), score(jnp.minimum(2 * j + 2, 15), 0))
         deliver(2 * j + 1)
@@ -286,19 +348,26 @@
     for a in range(2):
         wait(lk.at[0], lk_in.at[a])
         wait(lv.at[0], lv_in.at[a])
-    for h in range(4):
-        wait(rk.at[h], rk_in.at[h])
-        wait(rv.at[h], rv_in.at[h])
+
+    @pl.when(has_after)
+    def _():
+        for h in range(4):
+            wait(rk.at[h], rk_in.at[h])
+            wait(rv.at[h], rv_in.at[h])
+        wait(k_ref, send.at[0])
+        wait(v_ref, send.at[1])
+
+    @pl.when(has_before)
+    def _():
+        wait(hk, send.at[6])
+        wait(hv, send.at[7])
+
     wait(attn_ref, o_in)
     wait(dq_ref, dq_in)
-    wait(k_ref, send.at[0])
-    wait(v_ref, send.at[1])
     wait(k_ref.at[:, : 2 * HEAD], send.at[2])
     wait(v_ref.at[:, : 2 * HEAD], send.at[3])
     wait(q_ref.at[:, :, : 4 * HEAD], send.at[4])
     wait(g_ref.at[:, : 28 * HEAD], send.at[5])
-    wait(hk, send.at[6])
-    wait(hv, send.at[7])
     wait(out.at[:, :7], send.at[8])
     wait(dqs.at[:, :4], send.at[9])
     wait(pk, send.at[10])
@@ -362,7 +431,7 @@
             pltpu.VMEM((9, 128), jnp.int32),
             pltpu.VMEM((128, 16), jnp.int32),
             dma((12,)),
-            dma((2,)), dma((2,)), dma((2,)), dma((2,)), dma((2,)), dma((2,)),
+            dma((2,)), dma((2,)), dma((2,)), dma((2, 8)), dma((2, 8)), dma((2,)),
             dma(()), dma(()),
             dma((4,)), dma((4,)), dma((2,)), dma((2,)),
             dma(()), dma(()),

time: 53.3 us -> 50 us (0.938)
  Pallas kernels: 52.6 us -> 48.8 us
    pallas_call x1, Pallas kernels: 50.9 us -> 47.2 us  [body(): pl.pallas_call(kernel, out_shape=(attn_shape, dq_shape, part, part, part,...]
where the time goes in v3:
time: 50 us; the launch traced here: 49.5 us
  Pallas kernels  48.8 us (98%)
  between operations  0.64 us (1%)
    pallas_call x1, Pallas kernels, body(): pl.pallas_call(kernel, out_shape=(attn_shape, dq_shape, part, part, part,...  47.2 us
    pallas_call x1, Pallas kernels, body(): pl.pallas_call(finish, out_shape=(attn_shape, dq_shape, grad, grad), in_s...  1.69 us

profile of v3, /device:TPU:1, one launch (start us, length us, event | category | flops | bytes accessed | tf_op | source)
XLA Modules:
  0.0 49.5 jit_solution(2512952788646521347)
XLA Ops:
  0.6 47.2 %shard_map.93 = (bf16[128,4096]{1,0:T(8,128)(2,1)S(1)}, bf16[4,128,1024]{2,1,0:T(8,128)(2,1)S(1)}, bf16[4,512,128]{2,1,0:T(8,128)(2,1)S(1)}, bf16[4,512,128]{2,1...) custom-call(bf16[4,128,1024]{2,1,0:T(8,128)(2,1)} %bitcast.4, ...), custom_call_target="tpu_custom_call" | custom-call | tf_op jit(solution)/shard_map/pallas_call | solution.py:403
  47.8 1.7 %shard_map.94 = (bf16[128,4096]{1,0:T(8,128)(2,1)}, bf16[4,128,1024]{2,1,0:T(8,128)(2,1)}, bf16[512,512]{1,0:T(8,128)(2,1)}, bf16[512,512]{1,0:T(8,128)(2,1)}) custom-call(bf16[128,4096]{1,0:T(8,128)(2,1)S(1)} %get-tuple-element.14.attn_ref, bf16[4,128,1024]{2,1,0:T(8,128)(2,1)S(1)} %get-tuple-element.15.dq_ref, ...), custom_call_target="tpu_custom_call" | custom-call | tf_op jit(solution)/shard_map/pallas_call | solution.py:452

commit v4 on v3

--- a/solution.py
+++ b/solution.py
@@ -17,7 +17,7 @@
 ATTN_SCALE = 168.0 ** (-0.5)
 EXP2_SCALE = ATTN_SCALE * math.log2(math.e)
 NEG_FILL = -1e30
-ORDER = ((0, 1), (1, 0))
+ORDER = ((1, 0), (1, 0))
 FAR = 1 << 20
 
 MESH = pl.DeviceIdType.MESH
@@ -326,24 +326,22 @@
         pass
     wait(gs.at[0], g_in.at[0])
 
-    def loop(j, carry):
-        score_inputs(2 * j + 1)
-        interleave(grad(2 * j, 0), score(2 * j + 1, 1))
-        deliver(2 * j)
-
-        @pl.when(j == 3)
+    def loop(i, carry):
+        @pl.when(i < 15)
+        def _():
+            score_inputs(i + 1)
+
+        @pl.when(i == 7)
         def _():
             wait(gs.at[1], g_in.at[1])
 
-        @pl.when(j < 7)
-        def _():
-            score_inputs(2 * j + 2)
-
-        interleave(grad(2 * j + 1, 1), score(jnp.minimum(2 * j + 2, 15), 0))
-        deliver(2 * j + 1)
+        interleave(grad(i, 0), score(jnp.minimum(i + 1, 15), 1))
+        e_0[...] = e_1[...]
+        inv_0[...] = inv_1[...]
+        deliver(i)
         return carry
 
-    lax.fori_loop(0, 8, loop, 0)
+    lax.fori_loop(0, 16, loop, 0)
 
     for a in range(2):
         wait(lk.at[0], lk_in.at[a])

time: 50 us -> 48.2 us (0.964)
  Pallas kernels: 48.8 us -> 46.9 us
    pallas_call x1, Pallas kernels: 47.2 us -> 45.2 us  [body(): pl.pallas_call(kernel, out_shape=(attn_shape, dq_shape, part, part, part,...]
where the time goes in v4:
time: 48.2 us; the launch traced here: 47.6 us
  Pallas kernels  46.9 us (97%)
  between operations  0.64 us (1%)
    pallas_call x1, Pallas kernels, body(): pl.pallas_call(kernel, out_shape=(attn_shape, dq_shape, part, part, part,...  45.2 us
    pallas_call x1, Pallas kernels, body(): pl.pallas_call(finish, out_shape=(attn_shape, dq_shape, grad, grad), in_s...  1.69 us

profile of v4, /device:TPU:1, one launch (start us, length us, event | category | flops | bytes accessed | tf_op | source)
XLA Modules:
  0.0 47.6 jit_solution(15587690373751152295)
XLA Ops:
  0.6 45.2 %shard_map.93 = (bf16[128,4096]{1,0:T(8,128)(2,1)S(1)}, bf16[4,128,1024]{2,1,0:T(8,128)(2,1)S(1)}, bf16[4,512,128]{2,1,0:T(8,128)(2,1)S(1)}, bf16[4,512,128]{2,1...) custom-call(bf16[4,128,1024]{2,1,0:T(8,128)(2,1)} %bitcast.4, ...), custom_call_target="tpu_custom_call" | custom-call | tf_op jit(solution)/shard_map/pallas_call | solution.py:401
  45.9 1.7 %shard_map.94 = (bf16[128,4096]{1,0:T(8,128)(2,1)}, bf16[4,128,1024]{2,1,0:T(8,128)(2,1)}, bf16[512,512]{1,0:T(8,128)(2,1)}, bf16[512,512]{1,0:T(8,128)(2,1)}) custom-call(bf16[128,4096]{1,0:T(8,128)(2,1)S(1)} %get-tuple-element.14.attn_ref, bf16[4,128,1024]{2,1,0:T(8,128)(2,1)S(1)} %get-tuple-element.15.dq_ref, ...), custom_call_target="tpu_custom_call" | custom-call | tf_op jit(solution)/shard_map/pallas_call | solution.py:450

commit v5 on v4

--- a/solution.py
+++ b/solution.py
@@ -67,7 +67,7 @@
     g_t = (gs[a, p].T.astype(F32) * inv).astype(BF16)
     o_t = (dot(vt[a, :, window], e_scr[...], NN) * inv).astype(BF16)
     delta = jnp.sum(g_t.astype(F32) * o_t.astype(F32), axis=0, keepdims=True)
-    out[a, p] = o_t.T
+    out[a, p] = o_t.T.reshape(2, BLOCK, HEAD)
     yield
     for t in range(SPAN // TILE):
         rows = slice(t * TILE, (t + 1) * TILE)
@@ -79,24 +79,25 @@
         dv[a, key_rows, :] += dot(e, g_t, NT)
         dk[a, key_rows, :] += dot(ds, q, NN)
         yield
-    dq[a, p] = (dot(kt[a, :, window], d_scr[...], NN) * ATTN_SCALE).astype(BF16).T
+    grad_q = (dot(kt[a, :, window], d_scr[...], NN) * ATTN_SCALE).astype(BF16).T
+    dq[a, p] = grad_q.reshape(2, BLOCK, HEAD)
 
 
 def interleave(first, second):
     live = True
     while live:
         live = False
-        for chunks, times in ((first, 1), (second, 3)):
+        for chunks, times in ((first, 1), (second, 4)):
             for _ in range(times):
                 live = next(chunks, chunks) is not chunks or live
 
 
 def kernel(
     q_ref, k_ref, v_ref, g_ref, band_ref, seg_ref,
-    attn_ref, dq_ref, lk, lv, rk, rv,
+    attn_ref, dq_ref, lk, lv, rkv,
     qs, gs, kx, vx, kt, vt, low, out, dqs, dk, dv, s_scr, e_0, e_1, inv_0, inv_1, d_scr,
-    hk, hv, pk, pv, seg_v, band_v, band_t,
-    send, q_in, k_in, v_in, hk_in, hv_in, g_in, o_in, dq_in, rk_in, rv_in, lk_in, lv_in, seg_in, band_in,
+    hkv, pk, pv, seg_v, band_v, band_t,
+    send, q_in, k_in, v_in, hk_in, hv_in, g_in, o_in, dq_in, rkv_in, lk_in, lv_in, seg_in, band_in,
 ):
     me, x = lax.axis_index("ctx"), lax.axis_index("mp")
     chip, core = me // 2, me % 2
@@ -210,7 +211,7 @@
 
     def block_of(i):
         r = i % 8
-        return (r + 5) % 8 + (2 - 2 * r) * (1 - (r + 5) // 8)
+        return (r + 6) % 8 + (1 - 2 * r) * (1 - (r + 6) // 8)
 
     def take_halo(a, b):
         rows = pl.ds(pl.multiple_of(b * BLOCK, BLOCK), BLOCK)
@@ -225,17 +226,17 @@
     def score_inputs(i):
         a, r = i // 8, i % 8
 
-        @pl.when(r < 3)
+        @pl.when(r < 2)
         def _():
             take_halo(a, 7 - r)
 
-        @pl.when(r == 3)
+        @pl.when(r == 2)
         def _():
             def step(b, carry):
-                take_halo(a, 4 - b)
+                take_halo(a, 5 - b)
                 return carry
 
-            lax.fori_loop(0, 5, step, 0)
+            lax.fori_loop(0, 6, step, 0)
 
     @pl.when(chip == 0)
     def _():
@@ -245,8 +246,7 @@
 
     @pl.when(chip == CHIPS - 1)
     def _():
-        rk[...] = jnp.zeros_like(rk)
-        rv[...] = jnp.zeros_like(rv)
+        rkv[...] = jnp.zeros_like(rkv)
 
     dk[...] = jnp.zeros_like(dk)
     dv[...] = jnp.zeros_like(dv)
@@ -271,45 +271,41 @@
 
         def give(b, carry):
             rows = pl.ds(pl.multiple_of(b * BLOCK, BLOCK), BLOCK)
-            hk[a, b] = (dk[a, rows, :] * ATTN_SCALE).astype(BF16)
-            hv[a, b] = dv[a, rows, :].astype(BF16)
-            at_rows = pl.ds(pl.multiple_of((b % 4) * BLOCK, BLOCK), BLOCK)
+            hkv[a, b, 0] = (dk[a, rows, :] * ATTN_SCALE).astype(BF16)
+            hkv[a, b, 1] = dv[a, rows, :].astype(BF16)
             to = (2 * before + b // 4, x)
-            push(hk.at[a, b], rk.at[head, at_rows, :], 6, rk_in.at[head], to)
-            push(hv.at[a, b], rv.at[head, at_rows, :], 7, rv_in.at[head], to)
+            push(hkv.at[a, b], rkv.at[head, b % 4], 6, rkv_in.at[head], to)
             return carry
 
-        @pl.when(has_before & (r >= 3))
+        @pl.when(has_before & (r >= 2))
         def _():
             give(p, 0)
 
         @pl.when(has_before & (r == 7))
         def _():
-            lax.fori_loop(5, 8, give, 0)
-
-        for g in range(2):
-            part = slice(g * BLOCK, (g + 1) * BLOCK)
-            src = out.at[a, p, part, :]
-            dst = attn_ref.at[:, columns(x * 8 + core * 4 + 2 * a + g)]
-
-            @pl.when(p == my_block)
-            def _():
-                pltpu.make_async_copy(src, dst, o_in).start()
-
-            @pl.when(p != my_block)
-            def _():
-                push(src, dst, 8, o_in, (2 * chip + p // 4, p % 4))
-
-            src2 = dqs.at[a, p, part, :]
-            dst2 = dq_ref.at[p % 4, :, columns(2 * head + g)]
-
-            @pl.when(p // 4 == core)
-            def _():
-                pltpu.make_async_copy(src2, dst2, dq_in).start()
-
-            @pl.when(p // 4 != core)
-            def _():
-                push(src2, dst2, 9, dq_in, (mate, x))
+            lax.fori_loop(6, 8, give, 0)
+
+        src = out.at[a, p]
+        dst = attn_ref.at[pl.ds(x * 8 + core * 4 + 2 * a, 2)]
+
+        @pl.when(p == my_block)
+        def _():
+            pltpu.make_async_copy(src, dst, o_in).start()
+
+        @pl.when(p != my_block)
+        def _():
+            push(src, dst, 8, o_in, (2 * chip + p // 4, p % 4))
+
+        src2 = dqs.at[a, p]
+        dst2 = dq_ref.at[pl.ds(2 * head, 2), p % 4]
+
+        @pl.when(p // 4 == core)
+        def _():
+            pltpu.make_async_copy(src2, dst2, dq_in).start()
+
+        @pl.when(p // 4 != core)
+        def _():
+            push(src2, dst2, 9, dq_in, (mate, x))
 
         @pl.when(r == 7)
         def _():
@@ -350,15 +346,13 @@
     @pl.when(has_after)
     def _():
         for h in range(4):
-            wait(rk.at[h], rk_in.at[h])
-            wait(rv.at[h], rv_in.at[h])
+            wait(rkv.at[h], rkv_in.at[h])
         wait(k_ref, send.at[0])
         wait(v_ref, send.at[1])
 
     @pl.when(has_before)
     def _():
-        wait(hk, send.at[6])
-        wait(hv, send.at[7])
+        wait(hkv, send.at[6])
 
     wait(attn_ref, o_in)
     wait(dq_ref, dq_in)
@@ -372,20 +366,25 @@
     wait(pv, send.at[11])
 
 
-def finish(attn_ref, dq_ref, lk, lv, rk, rv, attn_out, dq_out, dk_out, dv_out, dk, dv, sems):
+def finish(attn_ref, dq_ref, lk, lv, rkv, attn_out, dq_out, dk_out, dv_out, dk, dv, sems):
+    for h in range(32):
+        cols = slice(h * HEAD, (h + 1) * HEAD)
+        pltpu.make_async_copy(attn_ref.at[h], attn_out.at[:, cols], sems.at[0]).start()
+    for h in range(8):
+        cols = slice(h * HEAD, (h + 1) * HEAD)
+        pltpu.make_async_copy(dq_ref.at[h], dq_out.at[:, :, cols], sems.at[1]).start()
     copies = [
-        pltpu.make_async_copy(attn_ref, attn_out, sems.at[0]),
-        pltpu.make_async_copy(dq_ref, dq_out, sems.at[1]),
         pltpu.make_async_copy(dk, dk_out, sems.at[2]),
         pltpu.make_async_copy(dv, dv_out, sems.at[3]),
     ]
-    copies[0].start()
-    copies[1].start()
-    for ours, other, total, copy in ((lk, rk, dk, copies[2]), (lv, rv, dv, copies[3])):
+    for which, ours, total in ((0, lk, dk), (1, lv, dv)):
         for h in range(4):
             cols = slice(h * HEAD, (h + 1) * HEAD)
-            total[:, cols] = (ours[h].astype(F32) + other[h].astype(F32)).astype(BF16)
-        copy.start()
+            other = rkv[h, :, which].reshape(4 * BLOCK, HEAD)
+            total[:, cols] = (ours[h].astype(F32) + other.astype(F32)).astype(BF16)
+        copies[which].start()
+    pltpu.make_async_copy(attn_ref, attn_ref, sems.at[0]).wait()
+    pltpu.make_async_copy(dq_ref, dq_ref, sems.at[1]).wait()
     for copy in copies:
         copy.wait()
 
@@ -395,14 +394,18 @@
     anywhere = pl.BlockSpec(memory_space=pl.ANY)
     vmem = pl.BlockSpec(memory_space=pltpu.VMEM)
     dma = pltpu.SemaphoreType.DMA
-    attn_shape = jax.ShapeDtypeStruct((128, 4096), BF16)
-    dq_shape = jax.ShapeDtypeStruct((4, 128, 1024), BF16)
     part = jax.ShapeDtypeStruct((4, 512, 128), BF16)
     pieces = pl.pallas_call(
         kernel,
-        out_shape=(attn_shape, dq_shape, part, part, part, part),
+        out_shape=(
+            jax.ShapeDtypeStruct((32, 128, 128), BF16),
+            jax.ShapeDtypeStruct((8, 4, 128, 128), BF16),
+            part,
+            part,
+            jax.ShapeDtypeStruct((4, 4, 2, 128, 128), BF16),
+        ),
         in_specs=[hbm] * 6,
-        out_specs=(anywhere, anywhere, vmem, vmem, vmem, vmem),
+        out_specs=(anywhere, anywhere, vmem, vmem, vmem),
         scratch_shapes=[
             pltpu.VMEM((2, 8, 256, 128), BF16),
             pltpu.VMEM((2, 8, 256, 128), BF16),
@@ -411,8 +414,8 @@
             pltpu.VMEM((2, 128, 2048), BF16),
             pltpu.VMEM((2, 128, 2048), BF16),
             pltpu.VMEM((9, 8, 256), jnp.int32),
-            pltpu.VMEM((2, 8, 256, 128), BF16),
-            pltpu.VMEM((2, 8, 256, 128), BF16),
+            pltpu.VMEM((2, 8, 2, 128, 128), BF16),
+            pltpu.VMEM((2, 8, 2, 128, 128), BF16),
             pltpu.VMEM((2, 2048, 128), F32),
             pltpu.VMEM((2, 2048, 128), F32),
             pltpu.VMEM((SPAN, 256), F32),
@@ -421,8 +424,7 @@
             pltpu.VMEM((8, 256), F32),
             pltpu.VMEM((8, 256), F32),
             pltpu.VMEM((SPAN, 256), BF16),
-            pltpu.VMEM((2, 8, 128, 128), BF16),
-            pltpu.VMEM((2, 8, 128, 128), BF16),
+            pltpu.VMEM((2, 8, 2, 128, 128), BF16),
             pltpu.VMEM((2, 512, 128), BF16),
             pltpu.VMEM((2, 512, 128), BF16),
             pltpu.VMEM((128, 128), jnp.int32),
@@ -431,7 +433,7 @@
             dma((12,)),
             dma((2,)), dma((2,)), dma((2,)), dma((2, 8)), dma((2, 8)), dma((2,)),
             dma(()), dma(()),
-            dma((4,)), dma((4,)), dma((2,)), dma((2,)),
+            dma((4,)), dma((2,)), dma((2,)),
             dma(()), dma(()),
         ],
         compiler_params=pltpu.CompilerParams(
@@ -449,8 +451,13 @@
     grad = jax.ShapeDtypeStruct((512, 512), BF16)
     attn, dq, dk, dv = pl.pallas_call(
         finish,
-        out_shape=(attn_shape, dq_shape, grad, grad),
-        in_specs=[anywhere, anywhere, vmem, vmem, vmem, vmem],
+        out_shape=(
+            jax.ShapeDtypeStruct((128, 4096), BF16),
+            jax.ShapeDtypeStruct((4, 128, 1024), BF16),
+            grad,
+            grad,
+        ),
+        in_specs=[anywhere, anywhere, vmem, vmem, vmem],
         out_specs=(hbm,) * 4,
         scratch_shapes=[pltpu.VMEM((512, 512), BF16), pltpu.VMEM((512, 512), BF16), dma((4,))],
         compiler_params=pltpu.CompilerParams(vmem_limit_bytes=16 << 20),

time: 48.2 us -> 47.9 us (level)
  the two profiles are of different devices: /device:TPU:1 before, /device:TPU:113 now
where the time goes in v5:
time: 47.9 us; the launch traced here: 47.8 us
  Pallas kernels  47.2 us (99%)
  between operations  0.64 us (1%)
    pallas_call x1, Pallas kernels, body(): pl.pallas_call(kernel, out_shape=(jax.ShapeDtypeStruct((32, 128, 128), BF...  45.5 us
    pallas_call x1, Pallas kernels, body(): pl.pallas_call(finish, out_shape=(jax.ShapeDtypeStruct((128, 4096), BF16)...  1.68 us

profile of v5, /device:TPU:113, one launch (start us, length us, event | category | flops | bytes accessed | tf_op | source)
XLA Modules:
  0.0 47.8 jit_solution(3896309365259599898)
XLA Ops:
  0.6 45.5 %shard_map.93 = (bf16[32,128,128]{2,1,0:T(8,128)(2,1)S(1)}, bf16[8,4,128,128]{3,2,1,0:T(8,128)(2,1)S(1)}, bf16[4,512,128]{2,1,0:T(8,128)(2,1)S(1)}, bf16[4,512,1...) custom-call(bf16[4,128,1024]{2,1,0:T(8,128)(2,1)} %bitcast.4, bf16[512,512]{1,0:T(8,128)(2,1)} %k_ref.1, ...), custom_call_target="tpu_custom_call" | custom-call | tf_op jit(solution)/shard_map/pallas_call | solution.py:398
  46.2 1.7 %shard_map.94 = (bf16[128,4096]{1,0:T(8,128)(2,1)}, bf16[4,128,1024]{2,1,0:T(8,128)(2,1)}, bf16[512,512]{1,0:T(8,128)(2,1)}, bf16[512,512]{1,0:T(8,128)(2,1)}) custom-call(bf16[32,128,128]{2,1,0:T(8,128)(2,1)S(1)} %get-tuple-element.13.attn_ref, bf16[8,4,128,128]{3,2,1,0:T(8,128)(2,1)S(1)} %get-tuple-element.14.dq_ref, ...), custom_call_target="tpu_custom_call" | custom-call | tf_op jit(solution)/shard_map/pallas_call | solution.py:452

commit v6 on v5

--- a/solution.py
+++ b/solution.py
@@ -73,7 +73,7 @@
         rows = slice(t * TILE, (t + 1) * TILE)
         key_rows = pl.ds(start + t * TILE, TILE)
         e = e_scr[rows, :]
-        ds = (e.astype(F32) * (dot(vx[a, key_rows, :], g_t, NN) - delta)).astype(BF16)
+        ds = e * (dot(vx[a, key_rows, :], g_t, NN) - delta).astype(BF16)
         d_scr[rows, :] = ds
         yield
         dv[a, key_rows, :] += dot(e, g_t, NT)

time: 47.9 us -> 47.6 us (level)
  no operation moved by 1% of the time
where the time goes in v6:
time: 47.6 us; the launch traced here: 47.5 us
  Pallas kernels  46.8 us (98%)
  between operations  0.64 us (1%)
    pallas_call x1, Pallas kernels, body(): pl.pallas_call(kernel, out_shape=(jax.ShapeDtypeStruct((32, 128, 128), BF...  45.2 us
    pallas_call x1, Pallas kernels, body(): pl.pallas_call(finish, out_shape=(jax.ShapeDtypeStruct((128, 4096), BF16)...  1.68 us

profile of v6, /device:TPU:113, one launch (start us, length us, event | category | flops | bytes accessed | tf_op | source)
XLA Modules:
  0.0 47.5 jit_solution(15239180144901049565)
XLA Ops:
  0.6 45.2 %shard_map.93 = (bf16[32,128,128]{2,1,0:T(8,128)(2,1)S(1)}, bf16[8,4,128,128]{3,2,1,0:T(8,128)(2,1)S(1)}, bf16[4,512,128]{2,1,0:T(8,128)(2,1)S(1)}, bf16[4,512,1...) custom-call(bf16[4,128,1024]{2,1,0:T(8,128)(2,1)} %bitcast.4, bf16[512,512]{1,0:T(8,128)(2,1)} %k_ref.1, ...), custom_call_target="tpu_custom_call" | custom-call | tf_op jit(solution)/shard_map/pallas_call | solution.py:398
  45.8 1.7 %shard_map.94 = (bf16[128,4096]{1,0:T(8,128)(2,1)}, bf16[4,128,1024]{2,1,0:T(8,128)(2,1)}, bf16[512,512]{1,0:T(8,128)(2,1)}, bf16[512,512]{1,0:T(8,128)(2,1)}) custom-call(bf16[32,128,128]{2,1,0:T(8,128)(2,1)S(1)} %get-tuple-element.13.attn_ref, bf16[8,4,128,128]{3,2,1,0:T(8,128)(2,1)S(1)} %get-tuple-element.14.dq_ref, ...), custom_call_target="tpu_custom_call" | custom-call | tf_op jit(solution)/shard_map/pallas_call | solution.py:452
